TPU v7x, 32 devices: a whole 2x2x4 slice. The times are simulated.
32 devices in a mesh: groups: 2 (over y), slab: 4 (over z), pencil: 2 (over x), comp: 2 (over core).
Axes of the slice: x: 2, y: 2, z: 4, core: 2. Of those that a mesh axis runs over, the one named last changes fastest.
Arguments:
- u_start: float32 [3, 64, 64, 512], P(None, ('groups', 'slab'), 'pencil', 'comp'), parts along dimension 1, may hold values from -6 to 6
- toughness: float32 [64, 64, 512], P(('groups', 'slab'), 'pencil', 'comp'), parts along dimension 0, may hold values from 0.3 to 1.5
- crack_label: int32 [64, 64, 512], P(('groups', 'slab'), 'pencil', 'comp'), parts along dimension 0, may hold values from 0 to 2
- obs_weight: bfloat16 [32, 64, 2, 4096], P('slab', 'pencil', 'comp'), may hold values from -0.75 to 0.75
- sensor_cell: int32 [4096], replicated, may hold values from 0 to 4095
Outputs:
- moved: float32 [3, 64, 64, 512], P(None, ('groups', 'slab'), 'pencil', 'comp'), parts along dimension 1
- damage: float32 [64, 64, 512], P(('groups', 'slab'), 'pencil', 'comp'), parts along dimension 0
- readings: float32 [3, 8192], P(None, 'groups'), parts along dimension 1
There are 2 independent parts, one for each index of `groups`. A program takes and returns all parts, laid end to end along the dimension named above; an argument that names none is the same for every part. Nothing has to cross between parts.
Inputs may be any that keep to these rules, and one draw needn't show every extreme that they name: `sensor_cell`: numbers cell blocks as (64 z + y) * 2 + h. `crack_label`: 0 intact, 1 partly cracked, 2 cracked.
All inputs are finite; a program needn't handle non-finite values.
Results may differ from a plain program's by a relative error of at most 0.003.
Values sent between devices are 32-bit elements; how exact they have to be, the bound alone decides.
No kernel may reach another device: no remote copies, remote signals or barrier semaphores. Data moves between devices by JAX's collectives and lax.ppermute only.
A program may use at most 128 MiB of HBM per device.

v0:
```python
import functools

import jax
import jax.numpy as jnp
from jax import lax
from jax.experimental import pallas as pl
from jax.experimental.pallas import tpu as pltpu
from jax.sharding import PartitionSpec as P


SHEAR_MODULUS = 1.0
LAME_FIRST = 1.5
RESIDUAL_STIFF = 0.001
TIME_DISP = 0.15
TIME_DAMAGE = 0.08
DAMAGE_LEVEL = 0.45
POINT_GAIN = 8.0
LANES = 128
SUB = 8
COS_THIRD = (
    0.5000000037331834,
    0.5773496613984853,
    -0.11109449276880777,
    0.05327935086024303,
    -0.031925412185213546,
    0.01960032102518762,
    -0.010237508432464154,
    0.003654119632233793,
    -0.0006260453394989179,
)
F32 = jnp.float32
VMEM_LIMIT = 24 * 1024 * 1024
VMEM = pl.BlockSpec(memory_space=pltpu.VMEM)


def positive_square_sum(m00, m11, m22, m01, m02, m12):
    mean = (m00 + m11 + m22) * (1.0 / 3.0)
    b00, b11, b22 = m00 - mean, m11 - mean, m22 - mean
    s01, s02, s12 = m01 * m01, m02 * m02, m12 * m12
    p2 = (b00 * b00 + b11 * b11 + b22 * b22) * (1.0 / 6.0) + (s01 + s02 + s12) * (1.0 / 3.0)
    det = b00 * (b11 * b22 - s12) + 2.0 * (m01 * m02) * m12 - b11 * s02 - b22 * s01
    mean2 = mean * mean
    whole = mean * (mean2 - 3.0 * p2) + det
    up = whole >= 0.0
    safe = jnp.maximum(p2, 1e-24)
    inv = lax.rsqrt(safe)
    p = safe * inv
    half = 0.25 * (det * inv) * (inv * inv)
    half = jnp.where(up, half, -half) + 0.5
    half = jnp.minimum(jnp.maximum(half, 0.0), 1.0)
    t = jnp.sqrt(half)
    c = jnp.full_like(t, COS_THIRD[-1])
    for value in COS_THIRD[-2::-1]:
        c = c * t + value
    pc = p * c
    lead = jnp.where(up, mean, -mean)
    largest = lead + 2.0 * pc
    square = largest * largest
    norm = 6.0 * p2 + 3.0 * mean2
    rest = lead - pc
    return jnp.where(
        up, jnp.where(rest > 0.0, norm, square), jnp.where(rest < 0.0, norm - square, 0.0)
    )


def sides(merged, fn):
    if merged:
        return [jnp.where(lax.axis_index("pencil") == 0, fn(1), fn(-1))]
    return [fn(1), fn(-1)]


def is_left():
    return lax.axis_index("comp") == 0


def pack_columns(tiles, out):
    Y = out.shape[0]
    left = is_left()
    lane = lax.broadcasted_iota(jnp.int32, (Y, LANES), 1)
    slot = jnp.where(left, (lane + 2) // 2 % (LANES // 2), lane // 2)
    acc = jnp.zeros((Y, LANES), F32)
    for entry, plane in enumerate(tiles):
        X = plane.shape[1]
        tile = jnp.where(left, plane[:, X - LANES : X], plane[:, 0:LANES])
        turned = pltpu.roll(tile, 2 * entry, 1) if entry else tile
        acc = jnp.where(slot == entry, turned, acc)
    out[...] = jnp.where(left, pltpu.roll(acc, 2, 1), acc)


def put_columns(u, d, out):
    Z = d.shape[0]
    pack_columns([u.at[c, z] for c in range(3) for z in range(Z)] + [d.at[z] for z in range(Z)], out)


def is_even():
    return lax.axis_index("slab") % 2 == 0


def put_planes(u, d, first, second):
    _, Z, _, _ = u.shape
    even = is_even()
    for c in range(3):
        up, down = u[c, Z - 2 : Z], u[c, 0:2]
        first[2 * c : 2 * c + 2] = jnp.where(even, up, down)
        second[2 * c : 2 * c + 2] = jnp.where(even, down, up)
    up, down = d[Z - 1], d[0]
    first[6] = jnp.where(even, up, down)
    second[6] = jnp.where(even, down, up)


def plane_readers(first, second):
    even = is_even()

    def low(*at):
        return jnp.where(even, second[at], first[at])

    def high(*at):
        return jnp.where(even, first[at], second[at])

    return low, high


def column_reader(packet):
    rows = packet.shape[0]
    left = is_left()
    lane = lax.broadcasted_iota(jnp.int32, (rows, LANES), 1)
    inside = jnp.where(left, lane, LANES - 1 - lane) < 2
    packet = jnp.where(left, packet, pltpu.roll(packet, LANES - 2, 1))

    def column(entry):
        shift = (LANES - 2 * entry) % LANES
        turned = pltpu.roll(packet, shift, 1) if shift else packet
        return jnp.where(inside, turned, 0.0)

    return column


def send_kernel(u, label, first, second, rows, sems):
    Z = label.shape[0]
    parity = lax.axis_index("slab") & 1
    copies = []
    for k, (out, side) in enumerate(((first, 1 - parity), (second, parity))):
        for c in range(3):
            copies.append(
                pltpu.make_async_copy(
                    u.at[c, pl.ds(side * (Z - 2), 2)], out.at[2 * c : 2 * c + 2], sems.at[k, c]
                )
            )
        copies.append(
            pltpu.make_async_copy(label.at[pl.ds(side * (Z - 1), 1)], rows.at[k], sems.at[k, 3])
        )
    for copy in copies:
        copy.start()
    for copy in copies:
        copy.wait()
    first[6] = DAMAGE_LEVEL * rows[0, 0].astype(F32)
    second[6] = DAMAGE_LEVEL * rows[1, 0].astype(F32)


def load_kernel(u_hbm, label_hbm, first, u, d, cols, label, sems):
    del first
    copies = [pltpu.make_async_copy(u_hbm.at[c], u.at[c], sems.at[c]) for c in range(3)]
    copies.append(pltpu.make_async_copy(label_hbm, label, sems.at[3]))
    for copy in copies:
        copy.start()
    copies[3].wait()
    d[...] = DAMAGE_LEVEL * label[...].astype(F32)
    for copy in copies[:3]:
        copy.wait()
    put_columns(u, d, cols)


def rows_kernel(merged, u, d, xh, *outs):
    _, _, Y, _ = u.shape
    for c in range(3):
        for layer in range(2):
            row = lambda s: u[c, :, Y - 2 + layer if s > 0 else layer, :]
            for ref, value in zip(outs, sides(merged, row)):
                ref[2 * c + layer] = value
    for ref, value in zip(outs, sides(merged, lambda s: d[:, Y - 1 if s > 0 else 0, :])):
        ref[6] = value
    corner = lambda s: xh[Y - 1 : Y, :] if s > 0 else xh[0:1, :]
    for ref, value in zip(outs, sides(merged, corner)):
        ref[7, 0:1, 0:LANES] = value


def near_planes(first, second):
    low, high = plane_readers(first, second)
    return [low(2 * c + 1) for c in range(3)] + [high(2 * c) for c in range(3)]


def corner_rows_kernel(merged, first, second, after, *outs):
    del after
    Y = first.shape[1]
    for k, plane in enumerate(near_planes(first, second)):
        edge = lambda s: plane[Y - 1 : Y, :] if s > 0 else plane[0:1, :]
        for ref, value in zip(outs, sides(merged, edge)):
            ref[k : k + 1, :] = value


def corner_columns_kernel(first, second, after, cols):
    del after
    pack_columns(near_planes(first, second), cols)


def row_keepers(merged):
    if not merged:
        return (lambda value: value), (lambda value: value)
    py = lax.axis_index("pencil")
    return (
        lambda value: jnp.where(py != 0, value, 0.0),
        lambda value: jnp.where(py == 0, value, 0.0),
    )


def lay_out_columns(u, d, xh, U, D):
    _, Z, Y, X = u.shape
    H = SUB
    column = column_reader(xh[...])
    for c in range(3):
        U[c, :, H : H + Y, 0:X] = u[c]
        for z in range(Z):
            U[c, z, H : H + Y, X : X + LANES] = column(c * Z + z)
    D[:, H : H + Y, 0:X] = d[...]
    for z in range(Z):
        D[z, H : H + Y, X : X + LANES] = column(3 * Z + z)


def lay_out_rows(merged, ylo, yhi, U, D):
    Z, X = D.shape[0], ylo.shape[2]
    Y, H = D.shape[1] - 2 * SUB, SUB
    low_of, high_of = row_keepers(merged)
    low_corner = column_reader(low_of(ylo[7, 0:1, 0:LANES]))
    high_corner = column_reader(high_of(yhi[7, 0:1, 0:LANES]))
    for c in range(3):
        for layer in range(2):
            low, high = low_of(ylo[2 * c + layer]), high_of(yhi[2 * c + layer])
            for z in range(Z):
                U[c, z, H - 2 + layer : H - 1 + layer, 0:X] = low[z : z + 1]
                U[c, z, H + Y + layer : H + Y + layer + 1, 0:X] = high[z : z + 1]
        for z in range(Z):
            U[c, z, H - 1 : H, X : X + LANES] = low_corner(c * Z + z)
            U[c, z, H + Y : H + Y + 1, X : X + LANES] = high_corner(c * Z + z)
    low, high = low_of(ylo[6]), high_of(yhi[6])
    for z in range(Z):
        D[z, H - 1 : H, 0:X] = low[z : z + 1]
        D[z, H + Y : H + Y + 1, 0:X] = high[z : z + 1]


def lay_out_face(merged, k, far, near, low_rows, high_rows, columns, F):
    Y, X = near(0).shape
    H = SUB
    low_of, high_of = row_keepers(merged)
    column = column_reader(columns[...])
    for c in range(3):
        F[c, 0, H : H + Y, 0:X] = far(c)
        F[c, 1, H : H + Y, 0:X] = near(c)
        F[c, 1, H : H + Y, X : X + LANES] = column(3 * k + c)
        row = 3 * k + c
        F[c, 1, H - 1 : H, 0:X] = low_of(low_rows[row : row + 1, :])
        F[c, 1, H + Y : H + Y + 1, 0:X] = high_of(high_rows[row : row + 1, :])


def ahead(value):
    return pltpu.roll(value, value.shape[-1] - 1, value.ndim - 1)


def behind(value):
    return pltpu.roll(value, 1, value.ndim - 1)


ZZ, ZY, ZX, YY, YX, XX = range(6)
PAIRS = ((ZZ, ZY, ZX), (ZY, YY, YX), (ZX, YX, XX))


def gradients(at, row, count):
    rows = slice(row, row + count)
    gz, gy, gx = [], [], []
    for c in range(3):
        mid = at(c, 0)
        gz.append(at(c, 1)[rows, :] - at(c, -1)[rows, :])
        gy.append(mid[row + 1 : row + count + 1, :] - mid[row - 1 : row + count - 1, :])
        value = mid[rows, :]
        gx.append(ahead(value) - behind(value))
    return gz, gy, gx


def stiffness(damage):
    keep = 1.0 - damage
    return 0.5 * (keep * keep + RESIDUAL_STIFF)


def energy_of(gz, gy, gx, X):
    cut = lambda value: value[:, 0:X]
    z0, y1, x2 = cut(gz[0]), cut(gy[1]), cut(gx[2])
    mzy = 0.5 * cut(gy[0] + gz[1])
    mzx = 0.5 * cut(gx[0] + gz[2])
    myx = 0.5 * cut(gx[1] + gy[2])
    squares = positive_square_sum(z0, y1, x2, mzy, mzx, myx)
    grow = jnp.maximum(z0 + y1 + x2, 0.0)
    return (0.25 * 0.5 * LAME_FIRST) * (grow * grow) + (0.25 * SHEAR_MODULUS) * squares


def new_damage(mid, below, above, t, energy, tough):
    X = tough.shape[-1]
    r = t * SUB
    value = mid[r : r + SUB, :]
    core = value[:, 0:X]
    lap = (
        below
        + above
        + mid[r + 1 : r + SUB + 1, 0:X]
        + mid[r - 1 : r + SUB - 1, 0:X]
        + (ahead(value) + behind(value))[:, 0:X]
        - 6.0 * core
    )
    return core + TIME_DAMAGE * (2.0 * (1.0 - core) * energy + tough * (lap - core))


def row_stress(at, damage_plane, S, Y, X):
    H = SUB
    for row in (H - 1, H + Y):
        gz, gy, gx = gradients(at, row, 1)
        h = stiffness(damage_plane[row : row + 1, :])
        total = LAME_FIRST * (gz[0] + gy[1] + gx[2])
        for key, value in (
            (ZY, gy[0] + gz[1]),
            (YY, total + 2.0 * gy[1]),
            (YX, gx[1] + gy[2]),
        ):
            S[key, row : row + 1, 0:X] = (h * value)[:, 0:X]


def tile_stress(at, damage_plane, S, t, X):
    rows = slice(t * SUB, t * SUB + SUB)
    gz, gy, gx = gradients(at, t * SUB, SUB)
    h = stiffness(damage_plane[rows, :])
    total = LAME_FIRST * (gz[0] + gy[1] + gx[2])
    S[ZZ, rows, 0:X] = (h * (total + 2.0 * gz[0]))[:, 0:X]
    S[YY, rows, 0:X] = (h * (total + 2.0 * gy[1]))[:, 0:X]
    S[ZY, rows, 0:X] = (h * (gy[0] + gz[1]))[:, 0:X]
    S[ZX, rows, :] = h * (gx[0] + gz[2])
    S[YX, rows, :] = h * (gx[1] + gy[2])
    S[XX, rows, :] = h * (total + 2.0 * gx[2])
    return gz, gy, gx


def side_stress(at, damage_plane, S, Y, X):
    for t in range(1, Y // SUB + 1):
        r = t * SUB
        rows, out = slice(r, r + SUB), slice(X, X + LANES)
        gz, gy, gx = [], [], []
        for c in range(3):
            mid = at(c, 0)
            gz.append(at(c, 1)[rows, out] - at(c, -1)[rows, out])
            gy.append(mid[r + 1 : r + SUB + 1, out] - mid[r - 1 : r + SUB - 1, out])
            value = mid[rows, :]
            gx.append((ahead(value) - behind(value))[:, out])
        h = stiffness(damage_plane[rows, out])
        total = LAME_FIRST * (gz[0] + gy[1] + gx[2])
        S[ZX, rows, out] = h * (gx[0] + gz[2])
        S[YX, rows, out] = h * (gx[1] + gy[2])
        S[XX, rows, out] = h * (total + 2.0 * gx[2])


def face_stress(at, damage, S, Y, X):
    for t in range(1, Y // SUB + 1):
        rows = slice(t * SUB, t * SUB + SUB)
        gz, gy, gx = gradients(at, t * SUB, SUB)
        h = stiffness(damage(slice((t - 1) * SUB, t * SUB)))
        total = LAME_FIRST * (gz[0] + gy[1] + gx[2])
        for key, value in (
            (ZZ, total + 2.0 * gz[0]),
            (ZY, gy[0] + gz[1]),
            (ZX, gx[0] + gz[2]),
        ):
            S[key, rows, 0:X] = h * value[:, 0:X]


def plane_moved(below, mid, above, u_plane, t, X):
    r = t * SUB
    rows = slice(r, r + SUB)
    out = []
    for c in range(3):
        kz, ky, kx = PAIRS[c]
        value = mid[kx, rows, :]
        force = (
            above[kz, rows, 0:X]
            - below[kz, rows, 0:X]
            + mid[ky, r + 1 : r + SUB + 1, 0:X]
            - mid[ky, r - 1 : r + SUB - 1, 0:X]
            + (ahead(value) - behind(value))[:, 0:X]
        )
        out.append(u_plane(c)[(t - 1) * SUB : t * SUB, :] + (0.5 * TIME_DISP) * force)
    return out


def row_sums(new):
    lane = lax.broadcasted_iota(jnp.int32, (SUB, LANES), 1)
    sums = [jnp.sum(value, axis=-1, keepdims=True) for value in new]
    return jnp.where(lane == 0, sums[0], jnp.where(lane == 1, sums[1], sums[2]))


def means_of(pool, X):
    return (pool * (1.0 / X)).T[0:SUB].astype(jnp.bfloat16)


def inner_tiles(z, tiles, U, D, S, tough, damage):
    X = tough.shape[2]
    for t in tiles:
        slopes = tile_stress(lambda c, dz: U.at[c, z + dz], D.at[z], S.at[z - 1], t, X)
        if damage:
            rows = slice(t * SUB, t * SUB + SUB)
            own = slice((t - 1) * SUB, t * SUB)
            (out,) = damage
            out[z - 1, own, :] = new_damage(
                D.at[z],
                D[z - 1, rows, 0:X],
                D[z + 1, rows, 0:X],
                t,
                energy_of(*slopes, X),
                tough[z, own, :],
            )


def middle_kernel(last, u, d, tough, xh, *rest):
    U, D, S, *damage = rest[-3 if last else -4 :]
    Z, Y, _ = tough.shape
    lay_out_columns(u, d, xh, U, D)

    @pl.loop(1, Z - 1)
    def _(z):
        inner_tiles(z, range(2, Y // SUB), U, D, S, tough, damage)


def inner_kernel(merged, tough, ylo, yhi, after, *refs):
    del after
    U, D, S, *damage = refs[len(refs) // 2 :]
    Z, Y, X = tough.shape
    lay_out_rows(merged, ylo, yhi, U, D)

    @pl.loop(1, Z - 1)
    def _(z):
        row_stress(lambda c, dz: U.at[c, z + dz], D.at[z], S.at[z - 1], Y, X)
        inner_tiles(z, (1, Y // SUB), U, D, S, tough, damage)


def moved_kernel(last, u, S, after, *rest):
    del after
    if last:
        weight, moved, part, pool = rest
    else:
        (moved,) = rest
    _, Z, Y, X = u.shape

    @pl.loop(2, Z - 2)
    def _(z):
        for t in range(1, Y // SUB + 1):
            own = slice((t - 1) * SUB, t * SUB)
            new = plane_moved(
                S.at[z - 2], S.at[z - 1], S.at[z], lambda c: u.at[c, z], t, X
            )
            for c in range(3):
                moved[c, z - 2, own, :] = new[c]
            if last:
                start = pl.multiple_of((z - 2) * Y + (t - 1) * SUB, SUB)
                pool[pl.ds(start, SUB), :] = row_sums(new)

    if last:
        means = means_of(pool[...], X)
        means = jnp.concatenate([means, means], axis=1)
        chunk = 8 * LANES
        for k in range(weight.shape[1] // chunk):
            cols = slice(k * chunk, (k + 1) * chunk)
            part[:, cols] = jnp.dot(means, weight[:, cols], preferred_element_type=F32)


def weights_kernel(Z, Y, weight, sensor, after, inner, outer):
    del after
    count = lax.axis_size("comp")
    spread = Y * lax.axis_size("pencil")
    index = lax.broadcasted_iota(jnp.int32, (Z * Y, 1), 0)
    plane = lax.axis_index("slab") * Z + index // Y
    row = lax.axis_index("pencil") * Y + index % Y
    ids = (plane * spread + row) * count + lax.axis_index("comp")
    chunk = 8 * LANES
    two, end = 2 * Y, (Z - 2) * Y
    middle = end - two
    inner[0:middle, :] = weight[two:end, :]
    outer[0:two, :] = weight[0:two, :]
    outer[two : 2 * two, :] = weight[end : end + two, :]
    for k in range(sensor.shape[1] // chunk):
        cols = slice(k * chunk, (k + 1) * chunk)
        picks = jnp.where(ids == sensor[:, cols], POINT_GAIN, 0.0).astype(jnp.bfloat16)
        inner[middle : 2 * middle, cols] = picks[two:end]
        outer[2 * two : 3 * two, cols] = picks[0:two]
        outer[3 * two : 4 * two, cols] = picks[end : end + two]


def edge_slopes(U, low, high, z, t, X):
    Z = U.shape[1]
    r = t * SUB
    rows = slice(r, r + SUB)
    own = slice((t - 1) * SUB, t * SUB)
    gz, gy, gx = [], [], []
    for c in range(3):
        below = low(2 * c + 1, own) if z == 0 else U[c, z - 1, rows, 0:X]
        above = high(2 * c, own) if z == Z - 1 else U[c, z + 1, rows, 0:X]
        gz.append(above - below)
        gy.append(U[c, z, r + 1 : r + SUB + 1, 0:X] - U[c, z, r - 1 : r + SUB - 1, 0:X])
        value = U[c, z, rows, :]
        gx.append((ahead(value) - behind(value))[:, 0:X])
    return gz, gy, gx


def edge_damage(D, low, high, z, t, slopes, tough):
    Z, X = D.shape[0], tough.shape[2]
    rows = slice(t * SUB, t * SUB + SUB)
    own = slice((t - 1) * SUB, t * SUB)
    below = low(6, own) if z == 0 else D[z - 1, rows, 0:X]
    above = high(6, own) if z == Z - 1 else D[z + 1, rows, 0:X]
    return new_damage(D.at[z], below, above, t, energy_of(*slopes, X), tough[z, own, :])


def edge_kernel(U, D, tough, first, second, S, *damage):
    Z, Y, X = tough.shape
    low, high = plane_readers(first, second)
    for k, z in enumerate((0, Z - 1)):
        for t in range(1, Y // SUB + 1):
            rows = slice(t * SUB, t * SUB + SUB)
            gz, gy, gx = edge_slopes(U, low, high, z, t, X)
            h = stiffness(D[z, rows, 0:X])
            total = LAME_FIRST * (gz[0] + gy[1] + gx[2])
            S[k, ZZ, rows, 0:X] = h * (total + 2.0 * gz[0])
            S[k, YY, rows, 0:X] = h * (total + 2.0 * gy[1])
            S[k, XX, rows, 0:X] = h * (total + 2.0 * gx[2])
            S[k, ZY, rows, 0:X] = h * (gy[0] + gz[1])
            S[k, ZX, rows, 0:X] = h * (gx[0] + gz[2])
            S[k, YX, rows, 0:X] = h * (gx[1] + gy[2])
            if damage:
                own = slice((t - 1) * SUB, t * SUB)
                damage[0][k, own, :] = edge_damage(D, low, high, z, t, (gz, gy, gx), tough)


def damage_kernel(U, D, tough, first, second, after, damage):
    del after
    Z, Y, X = tough.shape
    low, high = plane_readers(first, second)
    tiles = range(1, Y // SUB + 1)
    for z in (0, Z - 1):
        for t in tiles:
            own = slice((t - 1) * SUB, t * SUB)
            slopes = edge_slopes(U, low, high, z, t, X)
            damage[z, own, :] = edge_damage(D, low, high, z, t, slopes, tough)

    @pl.loop(1, Z - 1)
    def _(z):
        for t in tiles:
            r = t * SUB
            rows = slice(r, r + SUB)
            own = slice((t - 1) * SUB, t * SUB)
            gz, gy, gx = gradients(lambda c, dz: U.at[c, z + dz], r, SUB)
            damage[z, own, :] = new_damage(
                D.at[z],
                D[z - 1, rows, 0:X],
                D[z + 1, rows, 0:X],
                t,
                energy_of(gz, gy, gx, X),
                tough[z, own, :],
            )


def outer_kernel(merged, last, *refs):
    rest = list(refs)
    take = lambda k: [rest.pop(0) for _ in range(k)]
    u, first, second, low_rows, high_rows, columns, U, D, S, E_in = take(10)
    if last:
        inner_part, edge_rows = take(2)
        E, moved, part = take(3)
    else:
        inner_moved, inner_damage, edge_damage = take(3)
        E, moved, damage, cols, to_first, to_second = take(6)
    del E_in
    low_face, high_face, faces = take(3)
    if last:
        (pool,) = take(1)
    _, Z, Y, X = u.shape
    tiles = range(1, Y // SUB + 1)
    low, high = plane_readers(first, second)
    lay_out_face(
        merged, 0, lambda c: low(2 * c), lambda c: low(2 * c + 1), low_rows, high_rows, columns, low_face
    )
    lay_out_face(
        merged, 1, lambda c: high(2 * c + 1), lambda c: high(2 * c), low_rows, high_rows, columns, high_face
    )

    def at_plane(z):
        def at(c, dz):
            k = z + dz
            if k < 0:
                return low_face.at[c, 2 + k]
            if k >= Z:
                return high_face.at[c, Z + 1 - k]
            return U.at[c, k]

        return at

    face_stress(at_plane(-1), lambda own: low(6, own), faces.at[0], Y, X)
    face_stress(at_plane(Z), lambda own: high(6, own), faces.at[1], Y, X)
    for k, z in enumerate((0, Z - 1)):
        row_stress(at_plane(z), D.at[z], E.at[k], Y, X)
        side_stress(at_plane(z), D.at[z], E.at[k], Y, X)

    def stress(z):
        if z < 0:
            return faces.at[0]
        if z >= Z:
            return faces.at[1]
        if z == 0:
            return E.at[0]
        if z == Z - 1:
            return E.at[1]
        return S.at[z - 1]

    for k, z in enumerate((0, 1, Z - 2, Z - 1)):
        for t in tiles:
            own = slice((t - 1) * SUB, t * SUB)
            new = plane_moved(stress(z - 1), stress(z), stress(z + 1), lambda c: u.at[c, z], t, X)
            for c in range(3):
                moved[c, k if last else z, own, :] = new[c]
            if last:
                start = k * Y + (t - 1) * SUB
                pool[start : start + SUB, :] = row_sums(new)
    if last:
        means = means_of(pool[...], X)
        means = jnp.concatenate([means, means], axis=1)
        chunk = 8 * LANES
        sub = lax.broadcasted_iota(jnp.int32, (SUB, LANES), 0)
        for k in range(edge_rows.shape[1] // chunk):
            start = slice(k * chunk, (k + 1) * chunk)
            value = inner_part[:, start] + jnp.dot(
                means, edge_rows[:, start], preferred_element_type=F32
            )
            for c in range(3):
                tile = jnp.zeros((SUB, LANES), F32)
                for j in range(SUB):
                    piece = value[c : c + 1, j * LANES : (j + 1) * LANES]
                    tile = jnp.where(sub == j, piece, tile)
                part[c, k] = tile
    else:
        for c in range(3):
            moved[c, 2 : Z - 2] = inner_moved[c]
        damage[0] = edge_damage[0]
        damage[1 : Z - 1] = inner_damage[...]
        damage[Z - 1] = edge_damage[1]
        put_planes(moved, damage, to_first, to_second)
        put_columns(moved, damage, cols)


def fields_kernel(inner_moved, edge_moved, moved):
    Z = moved.shape[1]
    for c in range(3):
        moved[c, 0:2] = edge_moved[c, 0:2]
        moved[c, 2 : Z - 2] = inner_moved[c]
        moved[c, Z - 2 : Z] = edge_moved[c, 2:4]


def finish_kernel(*refs):
    out = refs[-1]
    total = refs[0][...]
    for ref in refs[1:-1]:
        total = total + ref[...]
    for c in range(3):
        for k in range(total.shape[1]):
            for j in range(SUB):
                start = (k * SUB + j) * LANES
                out[c : c + 1, start : start + LANES] = total[c, k, j : j + 1, :]


def call(kernel, outs, *args, scratch=(), in_specs=None, micros=1, alias=None):
    many = isinstance(outs, (list, tuple))
    return pl.pallas_call(
        kernel,
        out_shape=outs,
        in_specs=in_specs or [VMEM] * len(args),
        out_specs=[VMEM] * len(outs) if many else VMEM,
        scratch_shapes=list(scratch),
        compiler_params=pltpu.CompilerParams(vmem_limit_bytes=VMEM_LIMIT),
        cost_estimate=pl.CostEstimate(
            flops=0, bytes_accessed=micros * 3_000_000, transcendentals=0
        ),
        input_output_aliases=alias or {},
    )(*args)


def up_pairs(count):
    return [(i, i + 1) for i in range(count - 1)]


def down_pairs(count):
    return [(i + 1, i) for i in range(count - 1)]


def all_sum(value):
    for axis in ("comp", "pencil"):
        count = lax.axis_size(axis)
        bit = 1
        while bit < count:
            other = lax.ppermute(value, axis, [(i, i ^ bit) for i in range(count)])
            value = value + other
            bit *= 2
    count = lax.axis_size("slab")
    bit = 1
    while count // bit > 4:
        value = value + lax.ppermute(value, "slab", [(i, i ^ bit) for i in range(count)])
        bit *= 2
    terms = [value]
    for k in range(1, count // bit):
        terms.append(lax.ppermute(value, "slab", [(i, i ^ (k * bit)) for i in range(count)]))
    return terms


def local(u_start, toughness, crack_label, obs_weight, sensor_cell):
    Z, Y, X = toughness.shape
    slabs, pencils = lax.axis_size("slab"), lax.axis_size("pencil")
    if lax.axis_size("comp") != 2 or Z < 6 or Z % SUB or 8 * Z > LANES:
        raise ValueError("unsupported block")
    merged = pencils == 2
    n = 1 if merged else 2
    shape = jax.ShapeDtypeStruct
    field, vector = shape((Z, Y, X), F32), shape((3, Z, Y, X), F32)
    columns = shape((Y, LANES), F32)
    sensors = sensor_cell.shape[0]
    rows, lanes = Y + 2 * SUB, X + LANES
    y_up, y_down = up_pairs(pencils), down_pairs(pencils)
    y_pairs = [y_up + y_down] if merged else [y_up, y_down]
    margins = [
        shape((3, Z, rows, lanes), F32),
        shape((Z, rows, lanes), F32),
        shape((Z - 2, 6, rows, lanes), F32),
    ]
    scratch = [
        pltpu.VMEM((3, 2, rows, lanes), F32),
        pltpu.VMEM((3, 2, rows, lanes), F32),
        pltpu.VMEM((2, 3, rows, lanes), F32),
    ]
    edges = shape((2, 6, rows, lanes), F32)
    planes = shape((7, Y, X), F32)
    evens = [pair for pair in up_pairs(slabs) + down_pairs(slabs) if min(pair) % 2 == 0]
    odds = [pair for pair in up_pairs(slabs) + down_pairs(slabs) if min(pair) % 2 == 1]
    swap = [(0, 1), (1, 0)]
    hbm = pl.BlockSpec(memory_space=pltpu.HBM)
    starts = [
        pltpu.with_memory_space_constraint(value, pltpu.HBM) for value in (u_start, crack_label)
    ]
    to_first, to_second = call(
        send_kernel,
        [planes, planes],
        *starts,
        scratch=[pltpu.VMEM((2, 1, Y, X), jnp.int32), pltpu.SemaphoreType.DMA((2, 4))],
        in_specs=[hbm, hbm],
    )
    moved, damage, cols = call(
        load_kernel,
        [vector, field, columns],
        *starts,
        to_first,
        scratch=[pltpu.VMEM((Z, Y, X), jnp.int32), pltpu.SemaphoreType.DMA((4,))],
        in_specs=[hbm, hbm, VMEM],
    )
    for step in range(2):
        last = step == 1
        first = lax.ppermute(to_first, "slab", evens)
        second = lax.ppermute(to_second, "slab", odds)
        xh = lax.ppermute(cols, "comp", swap)
        out = call(
            functools.partial(rows_kernel, merged), [shape((8, Z, X), F32)] * n, moved, damage, xh
        )
        ys = [lax.ppermute(y, "pencil", pairs) for y, pairs in zip(out, y_pairs)]
        after = [out[0]]
        if not last:
            inner_rows, outer_rows = call(
                functools.partial(weights_kernel, Z, Y),
                [
                    shape((2 * (Z - 4) * Y, sensors), jnp.bfloat16),
                    shape((8 * Y, sensors), jnp.bfloat16),
                ],
                obs_weight.reshape(Z * Y, sensors),
                sensor_cell.reshape(1, sensors),
                out[0],
            )
            after.append(inner_rows)
        inner_outs = margins if last else margins + [shape((Z - 2, Y, X), F32)]
        middle = call(
            functools.partial(middle_kernel, last), inner_outs, moved, damage, toughness, xh, *after
        )

        def run_inner(after):
            args = [toughness, ys[0], ys[-1], after]
            return call(
                functools.partial(inner_kernel, merged),
                inner_outs,
                *args,
                *middle,
                micros=2,
                alias={len(args) + k: k for k in range(len(inner_outs))},
            )

        if last:
            inner = run_inner(xh)
        corner_rows = call(
            functools.partial(corner_rows_kernel, merged),
            [shape((SUB, X), F32)] * n,
            first,
            second,
            inner[2] if last else middle[2],
        )
        corner_columns = call(corner_columns_kernel, columns, first, second, corner_rows[0])
        if not last:
            inner = run_inner(corner_columns)
        U, D, S = inner[:3]
        args = [moved, S, corner_columns]
        outs = [shape((3, Z - 4, Y, X), F32)]
        if last:
            args.append(inner_rows)
            outs.append(shape((SUB, sensors), F32))
        inner_moved, *more = call(
            functools.partial(moved_kernel, last),
            outs,
            *args,
            scratch=[pltpu.VMEM(((Z - 4) * Y, LANES), F32)] if last else [],
        )
        if last:
            more.append(outer_rows)
        crows = [lax.ppermute(y, "pencil", pairs) for y, pairs in zip(corner_rows, y_pairs)]
        ccols = lax.ppermute(corner_columns, "comp", swap)
        E, *more_damage = call(
            edge_kernel,
            [edges] if last else [edges, shape((2, Y, X), F32)],
            U,
            D,
            toughness,
            first,
            second,
        )
        args = [moved, first, second, crows[0], crows[-1], ccols, U, D, S, E]
        if last:
            _, edge_moved, part = call(
                functools.partial(outer_kernel, merged, True),
                [
                    edges,
                    shape((3, 4, Y, X), F32),
                    shape((3, sensors // (SUB * LANES), SUB, LANES), F32),
                ],
                *args,
                *more,
                scratch=scratch + [pltpu.VMEM((4 * Y, LANES), F32)],
                alias={9: 0},
            )
            damage = call(damage_kernel, field, U, D, toughness, first, second, part, micros=2)
            moved = call(fields_kernel, vector, inner_moved, edge_moved)
        else:
            _, moved, damage, cols, to_first, to_second = call(
                functools.partial(outer_kernel, merged, False),
                [edges, vector, field, columns, planes, planes],
                *args,
                inner_moved,
                inner[3],
                *more_damage,
                scratch=scratch,
                alias={9: 0},
            )
    terms = all_sum(part)
    readings = call(finish_kernel, shape((3, sensors), F32), *terms)
    return moved, damage, readings


def solution(mesh):
    return jax.shard_map(
        local,
        mesh=mesh,
        in_specs=(
            P(None, ("groups", "slab"), "pencil", "comp"),
            P(("groups", "slab"), "pencil", "comp"),
            P(("groups", "slab"), "pencil", "comp"),
            P("slab", "pencil", "comp", None),
            P(),
        ),
        out_specs=(
            P(None, ("groups", "slab"), "pencil", "comp"),
            P(("groups", "slab"), "pencil", "comp"),
            P(None, "groups"),
        ),
        check_vma=False,
    )
```

profile of v0, /device:TPU:0, one launch (start us, length us, event | category | flops | bytes accessed | tf_op | source)
XLA Modules:
  0.0 48.0 jit_solution(14394275639778142735)
XLA Ops:
  0.7 1.2 %shard_map.76 = (f32[7,32,256]{2,1,0:T(8,128)S(1)}, f32[7,32,256]{2,1,0:T(8,128)S(1)}) custom-call(f32[3,8,32,256]{3,2,1,0:T(8,128)} %u_hbm.1, s32[8,32,256]{2,1,0:T(8,128)} %label_hbm.1), custom_call_target="tpu_custom_call" | custom-call | bytes 3000000 | tf_op jit(solution)/shard_map/pallas_call | solution.py:682
  1.9 0.7 %collective-permute-start.1 = (f32[7,32,256]{2,1,0:T(8,128)S(1)}, f32[7,32,256]{2,1,0:T(8,128)S(1)}, u32[]{:S(2)}, u32[]{:S(2)}) collective-permute-start(f32[7,32,256]{2,1,0:T(8,128)S(1)} %get-tuple-element.37), channel_id=1, source_target_pairs={{4,8},{8,4},{5,9},{9,5},{6,10},{10,6},{7,11},{11,7},{20,24},{24,20... | collective-permute-start | bytes 688136 | tf_op jit(solution)/shard_map/ppermute | solution.py:774
  2.6 5.9 %collective-permute-start = (f32[7,32,256]{2,1,0:T(8,128)S(1)}, f32[7,32,256]{2,1,0:T(8,128)S(1)}, u32[]{:S(2)}, u32[]{:S(2)}) collective-permute-start(f32[7,32,256]{2,1,0:T(8,128)S(1)} %get-tuple-element.35.first), channel_id=1, source_target_pairs={{0,4},{8,12},{4,0},{12,8},{1,5},{9,13},{5,1},{13,9},{2,6},{10,14},... | collective-permute-start | bytes 688136 | tf_op jit(solution)/shard_map/ppermute | solution.py:773
  8.5 1.5 %shard_map.77 = (f32[3,8,32,256]{3,2,1,0:T(8,128)S(1)}, f32[8,32,256]{2,1,0:T(8,128)S(1)}, f32[32,128]{1,0:T(8,128)S(1)}) custom-call(f32[3,8,32,256]{3,2,1,0:T(8,128)} %u_hbm.1, s32[8,32,256]{2,1,0:T(8,128)} %label_hbm.1, f32[7,32,256]{2,1,0:T(8,128)S(1)} %get-tuple-element.35.first), custom_call_target="tpu_custom_call" | custom-call | bytes 3000000 | tf_op jit(solution)/shard_map/pallas_call | solution.py:682
  10.1 1.2 %collective-permute-done.2.xh = f32[32,128]{1,0:T(8,128)S(1)} collective-permute-done((f32[32,128]{1,0:T(8,128)S(1)}, f32[32,128]{1,0:T(8,128)S(1)}, u32[]{:S(2)}, u32[]{:S(2)}) %collective-permute-start.2) | collective-permute-done | bytes 16416 | tf_op jit(solution)/shard_map/ppermute | solution.py:775
  11.4 1.6 %collective-permute-start.5 = (f32[8,8,256]{2,1,0:T(8,128)S(1)}, f32[8,8,256]{2,1,0:T(8,128)S(1)}, u32[]{:S(2)}, u32[]{:S(2)}) collective-permute-start(f32[8,8,256]{2,1,0:T(8,128)S(1)} %shard_map.78.after.rest_0_), channel_id=1, source_target_pairs={{0,2},{2,0},{1,3},{3,1},{4,6},{6,4},{5,7},{7,5},{8,10},{10,8},{9,1... | collective-permute-start | bytes 196616 | tf_op jit(solution)/shard_map/ppermute | solution.py:779
  13.4 1.4 %shard_map.80 = (f32[3,8,48,384]{3,2,1,0:T(8,128)S(1)}, f32[8,48,384]{2,1,0:T(8,128)S(1)}, f32[6,6,48,384]{3,2,1,0:T(8,128)S(1)}, f32[6,32,256]{2,1,0:T(8,128)S(1)}) custom-call(f32[3,8,32,256]{3,2,1,0:T(8,128)S(1)} %get-tuple-element.36.u.refs_0_, f32[8,32,256]{2,1,0:T(8,128)S(1)} %get-tuple-element.38.d, f32[8,32,256]{2,1,0:T(8,128)S(1)} %copy-done, ...), custom_call_target="tpu_custom_call" | custom-call | bytes 3000000 | tf_op jit(solution)/shard_map/pallas_call | solution.py:682
  15.1 0.6 %collective-permute-start.3 = (f32[8,256]{1,0:T(8,128)S(1)}, f32[8,256]{1,0:T(8,128)S(1)}, u32[]{:S(2)}, u32[]{:S(2)}) collective-permute-start(f32[8,256]{1,0:T(8,128)S(1)} %shard_map.81.after), channel_id=1, source_target_pairs={{0,2},{2,0},{1,3},{3,1},{4,6},{6,4},{5,7},{7,5},{8,10},{10,8},{9,1... | collective-permute-start | bytes 24584 | tf_op jit(solution)/shard_map/ppermute | solution.py:835
  15.7 1.4 %shard_map.83 = (f32[3,8,48,384]{3,2,1,0:T(8,128)S(1)}, f32[8,48,384]{2,1,0:T(8,128)S(1)}, f32[6,6,48,384]{3,2,1,0:T(8,128)S(1)}, f32[6,32,256]{2,1,0:T(8,128)S(1)}) custom-call(f32[8,32,256]{2,1,0:T(8,128)S(1)} %copy-done, f32[8,8,256]{2,1,0:T(8,128)S(1)} %collective-permute-done.5.ylo.yhi, ...), custom_call_target="tpu_custom_call", output_to_operand_aliasing={{0}: (4, {}), {1}: (5, {}), {2}: (6, {}), {3}: (7, {})} | custom-call | bytes 6000000 | tf_op jit(solution)/shard_map/pallas_call | solution.py:682
  17.1 0.6 %shard_map.85.refs_10_ = f32[3,4,32,256]{3,2,1,0:T(8,128)S(1)} custom-call(f32[3,8,32,256]{3,2,1,0:T(8,128)S(1)} %get-tuple-element.36.u.refs_0_, f32[6,6,48,384]{3,2,1,0:T(8,128)S(1)} %get-tuple-element.47.S.refs_8_, f32[32,128]{1,0:T(8,128)S(1)} %shard_map.82.after), custom_call_target="tpu_custom_call" | custom-call | bytes 3000000 | tf_op jit(solution)/shard_map/pallas_call | solution.py:682
  17.7 0.6 %shard_map.84 = (f32[2,6,48,384]{3,2,1,0:T(8,128)S(1)}, f32[2,32,256]{2,1,0:T(8,128)S(1)}) custom-call(f32[3,8,48,384]{3,2,1,0:T(8,128)S(1)} %get-tuple-element.45.U.refs_6_, f32[8,48,384]{2,1,0:T(8,128)S(1)} %get-tuple-element.46.D.refs_7_, f32[8,32,256]{2,1,0:T(8,128)S(1)} %copy-done, f32[7,32,256]{2,1,0:T(8,128)S(1)} %collective-permute-done.first.refs_1_, ...), custom_call_target="tpu_custom_call" | custom-call | bytes 3000000 | tf_op jit(solution)/shard_map/pallas_call | solution.py:682
  18.2 0.5 %collective-permute-done.3.refs_3_.refs_4_ = f32[8,256]{1,0:T(8,128)S(1)} collective-permute-done((f32[8,256]{1,0:T(8,128)S(1)}, f32[8,256]{1,0:T(8,128)S(1)}, u32[]{:S(2)}, u32[]{:S(2)}) %collective-permute-start.3) | collective-permute-done | bytes 8224 | tf_op jit(solution)/shard_map/ppermute | solution.py:835
  18.8 1.0 %shard_map.86 = (f32[2,6,48,384]{3,2,1,0:T(8,128)S(1)}, f32[3,8,32,256]{3,2,1,0:T(8,128)S(1)}, f32[8,32,256]{2,1,0:T(8,128)S(1)}, f32[32,128]{1,0:T(8,128)S(1)},...) custom-call(f32[3,8,32,256]{3,2,1,0:T(8,128)S(1)} %get-tuple-element.36.u.refs_0_, ...), custom_call_target="tpu_custom_call", output_to_operand_aliasing={{0}: (9, {})} | custom-call | bytes 3000000 | tf_op jit(solution)/shard_map/pallas_call | solution.py:682
  19.8 1.2 %collective-permute-start.8 = (f32[7,32,256]{2,1,0:T(8,128)S(1)}, f32[7,32,256]{2,1,0:T(8,128)S(1)}, u32[]{:S(2)}, u32[]{:S(2)}) collective-permute-start(f32[7,32,256]{2,1,0:T(8,128)S(1)} %get-tuple-element.58), channel_id=1, source_target_pairs={{0,4},{8,12},{4,0},{12,8},{1,5},{9,13},{5,1},{13,9},{2,6},{10,14},... | collective-permute-start | bytes 688136 | tf_op jit(solution)/shard_map/ppermute | solution.py:773
  21.0 0.7 %collective-permute-start.9 = (f32[7,32,256]{2,1,0:T(8,128)S(1)}, f32[7,32,256]{2,1,0:T(8,128)S(1)}, u32[]{:S(2)}, u32[]{:S(2)}) collective-permute-start(f32[7,32,256]{2,1,0:T(8,128)S(1)} %get-tuple-element.59), channel_id=1, source_target_pairs={{4,8},{8,4},{5,9},{9,5},{6,10},{10,6},{7,11},{11,7},{20,24},{24,20... | collective-permute-start | bytes 688136 | tf_op jit(solution)/shard_map/ppermute | solution.py:774
  21.7 1.2 %collective-permute-done.6.xh.after = f32[32,128]{1,0:T(8,128)S(1)} collective-permute-done((f32[32,128]{1,0:T(8,128)S(1)}, f32[32,128]{1,0:T(8,128)S(1)}, u32[]{:S(2)}, u32[]{:S(2)}) %collective-permute-start.6) | collective-permute-done | bytes 16416 | tf_op jit(solution)/shard_map/ppermute | solution.py:775
  22.9 1.1 %collective-permute-start.7 = (f32[8,8,256]{2,1,0:T(8,128)S(1)}, f32[8,8,256]{2,1,0:T(8,128)S(1)}, u32[]{:S(2)}, u32[]{:S(2)}) collective-permute-start(f32[8,8,256]{2,1,0:T(8,128)S(1)} %shard_map.87.rest_0_), channel_id=1, source_target_pairs={{0,2},{2,0},{1,3},{3,1},{4,6},{6,4},{5,7},{7,5},{8,10},{10,8},{9,1... | collective-permute-start | bytes 196616 | tf_op jit(solution)/shard_map/ppermute | solution.py:779
  24.1 0.9 %shard_map.88 = (f32[3,8,48,384]{3,2,1,0:T(8,128)S(1)}, f32[8,48,384]{2,1,0:T(8,128)S(1)}, f32[6,6,48,384]{3,2,1,0:T(8,128)S(1)}) custom-call(f32[3,8,32,256]{3,2,1,0:T(8,128)S(1)} %get-tuple-element.51.u.refs_0_, f32[8,32,256]{2,1,0:T(8,128)S(1)} %get-tuple-element.52.d, f32[8,32,256]{2,1,0:T(8,128)S(1)} %copy-done, ...), custom_call_target="tpu_custom_call" | custom-call | bytes 3000000 | tf_op jit(solution)/shard_map/pallas_call | solution.py:682
  25.0 2.3 %collective-permute-done.7.ylo.yhi = f32[8,8,256]{2,1,0:T(8,128)S(1)} collective-permute-done((f32[8,8,256]{2,1,0:T(8,128)S(1)}, f32[8,8,256]{2,1,0:T(8,128)S(1)}, u32[]{:S(2)}, u32[]{:S(2)}) %collective-permute-start.7) | collective-permute-done | bytes 65568 | tf_op jit(solution)/shard_map/ppermute | solution.py:779
  27.3 1.0 %shard_map.89 = (f32[3,8,48,384]{3,2,1,0:T(8,128)S(1)}, f32[8,48,384]{2,1,0:T(8,128)S(1)}, f32[6,6,48,384]{3,2,1,0:T(8,128)S(1)}) custom-call(f32[8,32,256]{2,1,0:T(8,128)S(1)} %copy-done, f32[8,8,256]{2,1,0:T(8,128)S(1)} %collective-permute-done.7.ylo.yhi, ...), custom_call_target="tpu_custom_call", output_to_operand_aliasing={{0}: (4, {}), {1}: (5, {}), {2}: (6, {})} | custom-call | bytes 6000000 | tf_op jit(solution)/shard_map/pallas_call | solution.py:682
  28.5 1.1 %collective-permute-start.10 = (f32[8,256]{1,0:T(8,128)S(1)}, f32[8,256]{1,0:T(8,128)S(1)}, u32[]{:S(2)}, u32[]{:S(2)}) collective-permute-start(f32[8,256]{1,0:T(8,128)S(1)} %shard_map.90.after), channel_id=1, source_target_pairs={{0,2},{2,0},{1,3},{3,1},{4,6},{6,4},{5,7},{7,5},{8,10},{10,8},{9,1... | collective-permute-start | bytes 24584 | tf_op jit(solution)/shard_map/ppermute | solution.py:835
  29.7 1.5 %shard_map.92 = (f32[3,4,32,256]{3,2,1,0:T(8,128)S(1)}, f32[8,4096]{1,0:T(8,128)S(1)}) custom-call(f32[3,8,32,256]{3,2,1,0:T(8,128)S(1)} %get-tuple-element.51.u.refs_0_, f32[6,6,48,384]{3,2,1,0:T(8,128)S(1)} %get-tuple-element.57.after.S.refs_8_, f32[32,128]{1,0:T(8,128)S(1)} %shard_map.91.after, bf16[256,4096]{1,0:T(8,128)(2,1)S(1)} %get-tuple-element.40.rest_1_.rest_0_), custom_call_target="tpu_custom_call" | custom-call | bytes 3000000 | tf_op jit(solution)/shard_map/pallas_call | solution.py:682
  31.4 0.8 %collective-permute-done.10.refs_3_.refs_4_ = f32[8,256]{1,0:T(8,128)S(1)} collective-permute-done((f32[8,256]{1,0:T(8,128)S(1)}, f32[8,256]{1,0:T(8,128)S(1)}, u32[]{:S(2)}, u32[]{:S(2)}) %collective-permute-start.10) | collective-permute-done | bytes 8224 | tf_op jit(solution)/shard_map/ppermute | solution.py:835
  32.3 1.4 %shard_map.94 = (f32[2,6,48,384]{3,2,1,0:T(8,128)S(1)}, f32[3,4,32,256]{3,2,1,0:T(8,128)S(1)}, f32[3,4,8,128]{3,2,1,0:T(8,128)S(1)}) custom-call(f32[3,8,32,256]{3,2,1,0:T(8,128)S(1)} %get-tuple-element.51.u.refs_0_, f32[7,32,256]{2,1,0:T(8,128)S(1)} %collective-permute-done.8.first.refs_1_, ...), custom_call_target="tpu_custom_call", output_to_operand_aliasing={{0}: (9, {})} | custom-call | bytes 3000000 | tf_op jit(solution)/shard_map/pallas_call | solution.py:682
  33.8 1.2 %collective-permute-done.12 = f32[3,4,8,128]{3,2,1,0:T(8,128)S(1)} collective-permute-done((f32[3,4,8,128]{3,2,1,0:T(8,128)S(1)}, f32[3,4,8,128]{3,2,1,0:T(8,128)S(1)}, u32[]{:S(2)}, u32[]{:S(2)}) %collective-permute-start.12) | collective-permute-done | bytes 49184 | tf_op jit(solution)/shard_map/ppermute | solution.py:709
  35.0 1.1 %collective-permute-start.13 = (f32[3,4,8,128]{3,2,1,0:T(8,128)S(1)}, f32[3,4,8,128]{3,2,1,0:T(8,128)S(1)}, u32[]{:S(2)}, u32[]{:S(2)}) collective-permute-start(f32[3,4,8,128]{3,2,1,0:T(8,128)S(1)} %add.6), channel_id=1, source_target_pairs={{0,2},{2,0},{1,3},{3,1},{4,6},{6,4},{5,7},{7,5},{8,10},{10,8},{9,1... | collective-permute-start | bytes 147464 | tf_op jit(solution)/shard_map/ppermute | solution.py:709
  36.1 3.0 %collective-permute-done.13 = f32[3,4,8,128]{3,2,1,0:T(8,128)S(1)} collective-permute-done((f32[3,4,8,128]{3,2,1,0:T(8,128)S(1)}, f32[3,4,8,128]{3,2,1,0:T(8,128)S(1)}, u32[]{:S(2)}, u32[]{:S(2)}) %collective-permute-start.13) | collective-permute-done | bytes 49184 | tf_op jit(solution)/shard_map/ppermute | solution.py:709
  39.2 1.4 %collective-permute-start.16 = (f32[3,4,8,128]{3,2,1,0:T(8,128)S(1)}, f32[3,4,8,128]{3,2,1,0:T(8,128)S(1)}, u32[]{:S(2)}, u32[]{:S(2)}) collective-permute-start(f32[3,4,8,128]{3,2,1,0:T(8,128)S(1)} %add.7.refs_0_), channel_id=1, source_target_pairs={{0,12},{4,8},{8,4},{12,0},{1,13},{5,9},{9,5},{13,1},{2,14},{6,10},... | collective-permute-start | bytes 147464 | tf_op jit(solution)/shard_map/ppermute | solution.py:719
  40.6 2.7 %collective-permute-start.15 = (f32[3,4,8,128]{3,2,1,0:T(8,128)S(1)}, f32[3,4,8,128]{3,2,1,0:T(8,128)S(1)}, u32[]{:S(2)}, u32[]{:S(2)}) collective-permute-start(f32[3,4,8,128]{3,2,1,0:T(8,128)S(1)} %add.7.refs_0_), channel_id=1, source_target_pairs={{0,8},{4,12},{8,0},{12,4},{1,9},{5,13},{9,1},{13,5},{2,10},{6,14},... | collective-permute-start | bytes 147464 | tf_op jit(solution)/shard_map/ppermute | solution.py:719
  43.6 0.9 %shard_map.95 = f32[3,8,32,256]{3,2,1,0:T(8,128)} custom-call(f32[3,4,32,256]{3,2,1,0:T(8,128)S(1)} %get-tuple-element.60.inner_moved, f32[3,4,32,256]{3,2,1,0:T(8,128)S(1)} %get-tuple-element.65.edge_moved), custom_call_target="tpu_custom_call" | custom-call | bytes 3000000 | tf_op jit(solution)/shard_map/pallas_call | solution.py:682
  44.5 2.8 %shard_map.96 = f32[8,32,256]{2,1,0:T(8,128)} custom-call(f32[3,8,48,384]{3,2,1,0:T(8,128)S(1)} %get-tuple-element.61.U.refs_6_, f32[8,48,384]{2,1,0:T(8,128)S(1)} %get-tuple-element.62.D.refs_7_, f32[8,32,256]{2,1,0:T(8,128)S(1)} %copy-done, f32[7,32,256]{2,1,0:T(8,128)S(1)} %collective-permute-done.8.first.refs_1_, ...), custom_call_target="tpu_custom_call" | custom-call | bytes 6000000 | tf_op jit(solution)/shard_map/pallas_call | solution.py:682
  47.4 0.7 %shard_map.97 = f32[3,4096]{1,0:T(4,128)} custom-call(f32[3,4,8,128]{3,2,1,0:T(8,128)S(1)} %add.7.refs_0_, f32[3,4,8,128]{3,2,1,0:T(8,128)S(1)} %collective-permute-done.14.refs_1_, f32[3,4,8,128]{3,2,1,0:T(8,128)S(1)} %collective-permute-done.15.refs_2_, f32[3,4,8,128]{3,2,1,0:T(8,128)S(1)} %collective-permute-done.16.refs_3_), custom_call_target="tpu_custom_call" | custom-call | bytes 3000000 | tf_op jit(solution)/shard_map/pallas_call | solution.py:682
  (32 shorter events, 1.9 us)
Async XLA Ops:
  0.6 12.3 %copy-start.2 = (s32[4096]{0:T(1024)S(1)}, s32[4096]{0:T(1024)}, u32[]{:S(2)}) copy-start(s32[4096]{0:T(1024)} %param.9) | copy-start | bytes 49156
  0.6 12.3 %copy-start.1 = (bf16[8,32,1,4096]{3,1,2,0:T(8,128)(2,1)S(1)}, bf16[8,32,1,4096]{3,1,2,0:T(8,128)(2,1)}, u32[]{:S(2)}) copy-start(bf16[8,32,1,4096]{3,1,2,0:T(8,128)(2,1)} %param.8) | copy-start | bytes 6291460
  1.9 12.9 %collective-permute-start.1 = (f32[7,32,256]{2,1,0:T(8,128)S(1)}, f32[7,32,256]{2,1,0:T(8,128)S(1)}, u32[]{:S(2)}, u32[]{:S(2)}) collective-permute-start(f32[7,32,256]{2,1,0:T(8,128)S(1)} %get-tuple-element.37), channel_id=1, source_target_pairs={{4,8},{8,4},{5,9},{9,5},{6,10},{10,6},{7,11},{11,7},{20,24},{24,20... | collective-permute-start | bytes 688136 | tf_op jit(solution)/shard_map/ppermute | solution.py:774
  2.6 10.8 %copy-start = (f32[8,32,256]{2,1,0:T(8,128)S(1)}, f32[8,32,256]{2,1,0:T(8,128)}, u32[]{:S(2)}) copy-start(f32[8,32,256]{2,1,0:T(8,128)} %tough.13) | copy-start | bytes 786436
  2.6 12.2 %collective-permute-start = (f32[7,32,256]{2,1,0:T(8,128)S(1)}, f32[7,32,256]{2,1,0:T(8,128)S(1)}, u32[]{:S(2)}, u32[]{:S(2)}) collective-permute-start(f32[7,32,256]{2,1,0:T(8,128)S(1)} %get-tuple-element.35.first), channel_id=1, source_target_pairs={{0,4},{8,12},{4,0},{12,8},{1,5},{9,13},{5,1},{13,9},{2,6},{10,14},... | collective-permute-start | bytes 688136 | tf_op jit(solution)/shard_map/ppermute | solution.py:773
  10.1 1.2 %collective-permute-start.2 = (f32[32,128]{1,0:T(8,128)S(1)}, f32[32,128]{1,0:T(8,128)S(1)}, u32[]{:S(2)}, u32[]{:S(2)}) collective-permute-start(f32[32,128]{1,0:T(8,128)S(1)} %get-tuple-element.39), channel_id=1, source_target_pairs={{0,1},{1,0},{2,3},{3,2},{4,5},{5,4},{6,7},{7,6},{8,9},{9,8},{10,11... | collective-permute-start | bytes 49160 | tf_op jit(solution)/shard_map/ppermute | solution.py:775
  11.4 4.3 %collective-permute-start.5 = (f32[8,8,256]{2,1,0:T(8,128)S(1)}, f32[8,8,256]{2,1,0:T(8,128)S(1)}, u32[]{:S(2)}, u32[]{:S(2)}) collective-permute-start(f32[8,8,256]{2,1,0:T(8,128)S(1)} %shard_map.78.after.rest_0_), channel_id=1, source_target_pairs={{0,2},{2,0},{1,3},{3,1},{4,6},{6,4},{5,7},{7,5},{8,10},{10,8},{9,1... | collective-permute-start | bytes 196616 | tf_op jit(solution)/shard_map/ppermute | solution.py:779
  15.0 3.7 %collective-permute-start.4 = (f32[32,128]{1,0:T(8,128)S(1)}, f32[32,128]{1,0:T(8,128)S(1)}, u32[]{:S(2)}, u32[]{:S(2)}) collective-permute-start(f32[32,128]{1,0:T(8,128)S(1)} %shard_map.82.after), channel_id=1, source_target_pairs={{0,1},{1,0},{2,3},{3,2},{4,5},{5,4},{6,7},{7,6},{8,9},{9,8},{10,11... | collective-permute-start | bytes 49160 | tf_op jit(solution)/shard_map/ppermute | solution.py:836
  15.1 3.7 %collective-permute-start.3 = (f32[8,256]{1,0:T(8,128)S(1)}, f32[8,256]{1,0:T(8,128)S(1)}, u32[]{:S(2)}, u32[]{:S(2)}) collective-permute-start(f32[8,256]{1,0:T(8,128)S(1)} %shard_map.81.after), channel_id=1, source_target_pairs={{0,2},{2,0},{1,3},{3,1},{4,6},{6,4},{5,7},{7,5},{8,10},{10,8},{9,1... | collective-permute-start | bytes 24584 | tf_op jit(solution)/shard_map/ppermute | solution.py:835
  19.8 8.5 %collective-permute-start.8 = (f32[7,32,256]{2,1,0:T(8,128)S(1)}, f32[7,32,256]{2,1,0:T(8,128)S(1)}, u32[]{:S(2)}, u32[]{:S(2)}) collective-permute-start(f32[7,32,256]{2,1,0:T(8,128)S(1)} %get-tuple-element.58), channel_id=1, source_target_pairs={{0,4},{8,12},{4,0},{12,8},{1,5},{9,13},{5,1},{13,9},{2,6},{10,14},... | collective-permute-start | bytes 688136 | tf_op jit(solution)/shard_map/ppermute | solution.py:773
  21.0 7.3 %collective-permute-start.9 = (f32[7,32,256]{2,1,0:T(8,128)S(1)}, f32[7,32,256]{2,1,0:T(8,128)S(1)}, u32[]{:S(2)}, u32[]{:S(2)}) collective-permute-start(f32[7,32,256]{2,1,0:T(8,128)S(1)} %get-tuple-element.59), channel_id=1, source_target_pairs={{4,8},{8,4},{5,9},{9,5},{6,10},{10,6},{7,11},{11,7},{20,24},{24,20... | collective-permute-start | bytes 688136 | tf_op jit(solution)/shard_map/ppermute | solution.py:774
  21.6 1.2 %collective-permute-start.6 = (f32[32,128]{1,0:T(8,128)S(1)}, f32[32,128]{1,0:T(8,128)S(1)}, u32[]{:S(2)}, u32[]{:S(2)}) collective-permute-start(f32[32,128]{1,0:T(8,128)S(1)} %get-tuple-element.53), channel_id=1, source_target_pairs={{0,1},{1,0},{2,3},{3,2},{4,5},{5,4},{6,7},{7,6},{8,9},{9,8},{10,11... | collective-permute-start | bytes 49160 | tf_op jit(solution)/shard_map/ppermute | solution.py:775
  22.9 4.3 %collective-permute-start.7 = (f32[8,8,256]{2,1,0:T(8,128)S(1)}, f32[8,8,256]{2,1,0:T(8,128)S(1)}, u32[]{:S(2)}, u32[]{:S(2)}) collective-permute-start(f32[8,8,256]{2,1,0:T(8,128)S(1)} %shard_map.87.rest_0_), channel_id=1, source_target_pairs={{0,2},{2,0},{1,3},{3,1},{4,6},{6,4},{5,7},{7,5},{8,10},{10,8},{9,1... | collective-permute-start | bytes 196616 | tf_op jit(solution)/shard_map/ppermute | solution.py:779
  28.5 3.7 %collective-permute-start.11 = (f32[32,128]{1,0:T(8,128)S(1)}, f32[32,128]{1,0:T(8,128)S(1)}, u32[]{:S(2)}, u32[]{:S(2)}) collective-permute-start(f32[32,128]{1,0:T(8,128)S(1)} %shard_map.91.after), channel_id=1, source_target_pairs={{0,1},{1,0},{2,3},{3,2},{4,5},{5,4},{6,7},{7,6},{8,9},{9,8},{10,11... | collective-permute-start | bytes 49160 | tf_op jit(solution)/shard_map/ppermute | solution.py:836
  28.5 3.7 %collective-permute-start.10 = (f32[8,256]{1,0:T(8,128)S(1)}, f32[8,256]{1,0:T(8,128)S(1)}, u32[]{:S(2)}, u32[]{:S(2)}) collective-permute-start(f32[8,256]{1,0:T(8,128)S(1)} %shard_map.90.after), channel_id=1, source_target_pairs={{0,2},{2,0},{1,3},{3,1},{4,6},{6,4},{5,7},{7,5},{8,10},{10,8},{9,1... | collective-permute-start | bytes 24584 | tf_op jit(solution)/shard_map/ppermute | solution.py:835
  33.7 1.3 %collective-permute-start.12 = (f32[3,4,8,128]{3,2,1,0:T(8,128)S(1)}, f32[3,4,8,128]{3,2,1,0:T(8,128)S(1)}, u32[]{:S(2)}, u32[]{:S(2)}) collective-permute-start(f32[3,4,8,128]{3,2,1,0:T(8,128)S(1)} %get-tuple-element.66.after), channel_id=1, source_target_pairs={{0,1},{1,0},{2,3},{3,2},{4,5},{5,4},{6,7},{7,6},{8,9},{9,8},{10,11... | collective-permute-start | bytes 147464 | tf_op jit(solution)/shard_map/ppermute | solution.py:709
  35.0 4.2 %collective-permute-start.13 = (f32[3,4,8,128]{3,2,1,0:T(8,128)S(1)}, f32[3,4,8,128]{3,2,1,0:T(8,128)S(1)}, u32[]{:S(2)}, u32[]{:S(2)}) collective-permute-start(f32[3,4,8,128]{3,2,1,0:T(8,128)S(1)} %add.6), channel_id=1, source_target_pairs={{0,2},{2,0},{1,3},{3,1},{4,6},{6,4},{5,7},{7,5},{8,10},{10,8},{9,1... | collective-permute-start | bytes 147464 | tf_op jit(solution)/shard_map/ppermute | solution.py:709
  39.2 8.2 %collective-permute-start.16 = (f32[3,4,8,128]{3,2,1,0:T(8,128)S(1)}, f32[3,4,8,128]{3,2,1,0:T(8,128)S(1)}, u32[]{:S(2)}, u32[]{:S(2)}) collective-permute-start(f32[3,4,8,128]{3,2,1,0:T(8,128)S(1)} %add.7.refs_0_), channel_id=1, source_target_pairs={{0,12},{4,8},{8,4},{12,0},{1,13},{5,9},{9,5},{13,1},{2,14},{6,10},... | collective-permute-start | bytes 147464 | tf_op jit(solution)/shard_map/ppermute | solution.py:719
  40.6 6.8 %collective-permute-start.15 = (f32[3,4,8,128]{3,2,1,0:T(8,128)S(1)}, f32[3,4,8,128]{3,2,1,0:T(8,128)S(1)}, u32[]{:S(2)}, u32[]{:S(2)}) collective-permute-start(f32[3,4,8,128]{3,2,1,0:T(8,128)S(1)} %add.7.refs_0_), channel_id=1, source_target_pairs={{0,8},{4,12},{8,0},{12,4},{1,9},{5,13},{9,1},{13,5},{2,10},{6,14},... | collective-permute-start | bytes 147464 | tf_op jit(solution)/shard_map/ppermute | solution.py:719
  43.2 4.1 %collective-permute-start.14 = (f32[3,4,8,128]{3,2,1,0:T(8,128)S(1)}, f32[3,4,8,128]{3,2,1,0:T(8,128)S(1)}, u32[]{:S(2)}, u32[]{:S(2)}) collective-permute-start(f32[3,4,8,128]{3,2,1,0:T(8,128)S(1)} %add.7.refs_0_), channel_id=1, source_target_pairs={{0,4},{4,0},{8,12},{12,8},{1,5},{5,1},{9,13},{13,9},{2,6},{6,2},{1... | collective-permute-start | bytes 147464 | tf_op jit(solution)/shard_map/ppermute | solution.py:719
where the time goes:
time: 48.2 us; the launch traced here: 48 us
  starting transfers between devices  18.7 us (39%)
  Pallas kernels  18.2 us (38%)
  waiting for transfers between devices  10.3 us (21%)
  between operations  0.85 us (2%)
    pallas_call x22, Pallas kernels, call(): pl.pallas_call(kernel, out_shape=outs, in_specs=in_specs or [VMEM] * len(...  18.2 us
    ppermute x2, starting transfers between devices, local(): first = lax.ppermute(to_first, 'slab', evens)  7.1 us
    ppermute x3, starting transfers between devices, all_sum(): lax.ppermute(value, 'slab', [(i, i ^ k * bit) for i in range(count)])  4.45 us
    ppermute x2, waiting for transfers between devices, all_sum(): other = lax.ppermute(value, axis, [(i, i ^ bit) for i in range(count)])  4.23 us
    ppermute x2, starting transfers between devices, local(): ys = [lax.ppermute(y, 'pencil', pairs) for y, pairs in zip(out, y_pairs)]  2.69 us
    ppermute x2, waiting for transfers between devices, local(): xh = lax.ppermute(cols, 'comp', swap)  2.34 us
    ppermute x2, waiting for transfers between devices, local(): ys = [lax.ppermute(y, 'pencil', pairs) for y, pairs in zip(out, y_pairs)]  2.29 us
    ppermute x2, starting transfers between devices, local(): lax.ppermute(y, 'pencil', pairs)  1.74 us
  transfers between devices with their start and end apart: 17, of which 7 were waited for; matrix products, arithmetic and copies ran while one was open for 0% of the time, Pallas kernels for 28%

commit v1 on v0

--- a/solution.py
+++ b/solution.py
@@ -135,30 +135,7 @@
     return column
 
 
-def send_kernel(u, label, first, second, rows, sems):
-    Z = label.shape[0]
-    parity = lax.axis_index("slab") & 1
-    copies = []
-    for k, (out, side) in enumerate(((first, 1 - parity), (second, parity))):
-        for c in range(3):
-            copies.append(
-                pltpu.make_async_copy(
-                    u.at[c, pl.ds(side * (Z - 2), 2)], out.at[2 * c : 2 * c + 2], sems.at[k, c]
-                )
-            )
-        copies.append(
-            pltpu.make_async_copy(label.at[pl.ds(side * (Z - 1), 1)], rows.at[k], sems.at[k, 3])
-        )
-    for copy in copies:
-        copy.start()
-    for copy in copies:
-        copy.wait()
-    first[6] = DAMAGE_LEVEL * rows[0, 0].astype(F32)
-    second[6] = DAMAGE_LEVEL * rows[1, 0].astype(F32)
-
-
-def load_kernel(u_hbm, label_hbm, first, u, d, cols, label, sems):
-    del first
+def load_kernel(u_hbm, label_hbm, u, d, first, second, label, sems):
     copies = [pltpu.make_async_copy(u_hbm.at[c], u.at[c], sems.at[c]) for c in range(3)]
     copies.append(pltpu.make_async_copy(label_hbm, label, sems.at[3]))
     for copy in copies:
@@ -167,6 +144,11 @@
     d[...] = DAMAGE_LEVEL * label[...].astype(F32)
     for copy in copies[:3]:
         copy.wait()
+    put_planes(u, d, first, second)
+
+
+def columns_kernel(u, d, first, cols):
+    del first
     put_columns(u, d, cols)
 
 
@@ -395,14 +377,21 @@
     return out
 
 
-def row_sums(new):
-    lane = lax.broadcasted_iota(jnp.int32, (SUB, LANES), 1)
-    sums = [jnp.sum(value, axis=-1, keepdims=True) for value in new]
-    return jnp.where(lane == 0, sums[0], jnp.where(lane == 1, sums[1], sums[2]))
-
-
-def means_of(pool, X):
-    return (pool * (1.0 / X)).T[0:SUB].astype(jnp.bfloat16)
+def put_folded(pool, start, new):
+    for c, value in enumerate(new):
+        total = value[:, 0:LANES]
+        for k in range(1, value.shape[1] // LANES):
+            total = total + value[:, k * LANES : (k + 1) * LANES]
+        pool[c, start : start + SUB, :] = total
+
+
+def sums_of(pool):
+    rows = pool.shape[1]
+    sub = lax.broadcasted_iota(jnp.int32, (SUB, rows), 0)
+    out = jnp.zeros((SUB, rows), F32)
+    for c in range(3):
+        out = jnp.where(sub == c, jnp.sum(pool[c].T, axis=0, keepdims=True), out)
+    return out
 
 
 def inner_tiles(z, tiles, U, D, S, tough, damage):
@@ -428,7 +417,7 @@
     Z, Y, _ = tough.shape
     lay_out_columns(u, d, xh, U, D)
 
-    @pl.loop(1, Z - 1)
+    @pl.loop(1, Z - 1, unroll=True)
     def _(z):
         inner_tiles(z, range(2, Y // SUB), U, D, S, tough, damage)
 
@@ -439,22 +428,16 @@
     Z, Y, X = tough.shape
     lay_out_rows(merged, ylo, yhi, U, D)
 
-    @pl.loop(1, Z - 1)
+    @pl.loop(1, Z - 1, unroll=True)
     def _(z):
         row_stress(lambda c, dz: U.at[c, z + dz], D.at[z], S.at[z - 1], Y, X)
         inner_tiles(z, (1, Y // SUB), U, D, S, tough, damage)
 
 
-def moved_kernel(last, u, S, after, *rest):
+def moved_kernel(last, u, S, after, moved, *more):
     del after
-    if last:
-        weight, moved, part, pool = rest
-    else:
-        (moved,) = rest
     _, Z, Y, X = u.shape
-
-    @pl.loop(2, Z - 2)
-    def _(z):
+    for z in range(2, Z - 2):
         for t in range(1, Y // SUB + 1):
             own = slice((t - 1) * SUB, t * SUB)
             new = plane_moved(
@@ -463,20 +446,14 @@
             for c in range(3):
                 moved[c, z - 2, own, :] = new[c]
             if last:
-                start = pl.multiple_of((z - 2) * Y + (t - 1) * SUB, SUB)
-                pool[pl.ds(start, SUB), :] = row_sums(new)
-
+                put_folded(more[1], (z - 2) * Y + (t - 1) * SUB, new)
     if last:
-        means = means_of(pool[...], X)
-        means = jnp.concatenate([means, means], axis=1)
-        chunk = 8 * LANES
-        for k in range(weight.shape[1] // chunk):
-            cols = slice(k * chunk, (k + 1) * chunk)
-            part[:, cols] = jnp.dot(means, weight[:, cols], preferred_element_type=F32)
-
-
-def weights_kernel(Z, Y, weight, sensor, after, inner, outer):
-    del after
+        sums, pool = more
+        sums[...] = sums_of(pool)
+
+
+def picks_kernel(Z, Y, sensor, weight, after, picks):
+    del weight, after
     count = lax.axis_size("comp")
     spread = Y * lax.axis_size("pencil")
     index = lax.broadcasted_iota(jnp.int32, (Z * Y, 1), 0)
@@ -484,17 +461,10 @@
     row = lax.axis_index("pencil") * Y + index % Y
     ids = (plane * spread + row) * count + lax.axis_index("comp")
     chunk = 8 * LANES
-    two, end = 2 * Y, (Z - 2) * Y
-    middle = end - two
-    inner[0:middle, :] = weight[two:end, :]
-    outer[0:two, :] = weight[0:two, :]
-    outer[two : 2 * two, :] = weight[end : end + two, :]
     for k in range(sensor.shape[1] // chunk):
         cols = slice(k * chunk, (k + 1) * chunk)
-        picks = jnp.where(ids == sensor[:, cols], POINT_GAIN, 0.0).astype(jnp.bfloat16)
-        inner[middle : 2 * middle, cols] = picks[two:end]
-        outer[2 * two : 3 * two, cols] = picks[0:two]
-        outer[3 * two : 4 * two, cols] = picks[end : end + two]
+        hit = ids == sensor[:, cols]
+        picks[:, cols] = jnp.where(hit, POINT_GAIN, 0.0).astype(jnp.bfloat16)
 
 
 def edge_slopes(U, low, high, z, t, X):
@@ -522,8 +492,9 @@
     return new_damage(D.at[z], below, above, t, energy_of(*slopes, X), tough[z, own, :])
 
 
-def edge_kernel(U, D, tough, first, second, S, *damage):
+def edge_kernel(last, u, inner, U, D, tough, first, second, S, moved, *more):
     Z, Y, X = tough.shape
+    pool, damage = (more, ()) if last else ((), more)
     low, high = plane_readers(first, second)
     for k, z in enumerate((0, Z - 1)):
         for t in range(1, Y // SUB + 1):
@@ -540,6 +511,18 @@
             if damage:
                 own = slice((t - 1) * SUB, t * SUB)
                 damage[0][k, own, :] = edge_damage(D, low, high, z, t, (gz, gy, gx), tough)
+    around = (
+        (1, S.at[0], inner.at[0], inner.at[1]),
+        (Z - 2, inner.at[Z - 4], inner.at[Z - 3], S.at[1]),
+    )
+    for k, (z, below, mid, above) in enumerate(around):
+        for t in range(1, Y // SUB + 1):
+            own = slice((t - 1) * SUB, t * SUB)
+            new = plane_moved(below, mid, above, lambda c: u.at[c, z], t, X)
+            for c in range(3):
+                moved[c, k, own, :] = new[c]
+            if last:
+                put_folded(pool[0], k * Y + (t - 1) * SUB, new)
 
 
 def damage_kernel(U, D, tough, first, second, after, damage):
@@ -553,7 +536,7 @@
             slopes = edge_slopes(U, low, high, z, t, X)
             damage[z, own, :] = edge_damage(D, low, high, z, t, slopes, tough)
 
-    @pl.loop(1, Z - 1)
+    @pl.loop(1, Z - 1, unroll=True)
     def _(z):
         for t in tiles:
             r = t * SUB
@@ -575,10 +558,10 @@
     take = lambda k: [rest.pop(0) for _ in range(k)]
     u, first, second, low_rows, high_rows, columns, U, D, S, E_in = take(10)
     if last:
-        inner_part, edge_rows = take(2)
+        inner_sums, near_pool, weight, picks = take(4)
         E, moved, part = take(3)
     else:
-        inner_moved, inner_damage, edge_damage = take(3)
+        inner_moved, near_moved, inner_damage, edge_damage = take(4)
         E, moved, damage, cols, to_first, to_second = take(6)
     del E_in
     low_face, high_face, faces = take(3)
@@ -622,25 +605,27 @@
             return E.at[1]
         return S.at[z - 1]
 
-    for k, z in enumerate((0, 1, Z - 2, Z - 1)):
+    for k, z in enumerate((0, Z - 1)):
         for t in tiles:
             own = slice((t - 1) * SUB, t * SUB)
             new = plane_moved(stress(z - 1), stress(z), stress(z + 1), lambda c: u.at[c, z], t, X)
             for c in range(3):
                 moved[c, k if last else z, own, :] = new[c]
             if last:
-                start = k * Y + (t - 1) * SUB
-                pool[start : start + SUB, :] = row_sums(new)
+                put_folded(pool, 3 * k * Y + (t - 1) * SUB, new)
     if last:
-        means = means_of(pool[...], X)
-        means = jnp.concatenate([means, means], axis=1)
+        pool[:, Y : 3 * Y, :] = near_pool[...]
+        outer_sums = sums_of(pool)
+        means = jnp.concatenate(
+            [outer_sums[:, 0 : 2 * Y], inner_sums[...], outer_sums[:, 2 * Y : 4 * Y]], axis=1
+        )
+        means = (means * (1.0 / X)).astype(jnp.bfloat16)
         chunk = 8 * LANES
         sub = lax.broadcasted_iota(jnp.int32, (SUB, LANES), 0)
-        for k in range(edge_rows.shape[1] // chunk):
+        for k in range(weight.shape[1] // chunk):
             start = slice(k * chunk, (k + 1) * chunk)
-            value = inner_part[:, start] + jnp.dot(
-                means, edge_rows[:, start], preferred_element_type=F32
-            )
+            value = jnp.dot(means, weight[:, start], preferred_element_type=F32)
+            value = value + jnp.dot(means, picks[:, start], preferred_element_type=F32)
             for c in range(3):
                 tile = jnp.zeros((SUB, LANES), F32)
                 for j in range(SUB):
@@ -649,7 +634,9 @@
                 part[c, k] = tile
     else:
         for c in range(3):
+            moved[c, 1] = near_moved[c, 0]
             moved[c, 2 : Z - 2] = inner_moved[c]
+            moved[c, Z - 2] = near_moved[c, 1]
         damage[0] = edge_damage[0]
         damage[1 : Z - 1] = inner_damage[...]
         damage[Z - 1] = edge_damage[1]
@@ -657,12 +644,14 @@
         put_columns(moved, damage, cols)
 
 
-def fields_kernel(inner_moved, edge_moved, moved):
+def fields_kernel(inner_moved, near_moved, edge_moved, moved):
     Z = moved.shape[1]
     for c in range(3):
-        moved[c, 0:2] = edge_moved[c, 0:2]
+        moved[c, 0] = edge_moved[c, 0]
+        moved[c, 1] = near_moved[c, 0]
         moved[c, 2 : Z - 2] = inner_moved[c]
-        moved[c, Z - 2 : Z] = edge_moved[c, 2:4]
+        moved[c, Z - 2] = near_moved[c, 1]
+        moved[c, Z - 1] = edge_moved[c, 1]
 
 
 def finish_kernel(*refs):
@@ -749,25 +738,19 @@
     evens = [pair for pair in up_pairs(slabs) + down_pairs(slabs) if min(pair) % 2 == 0]
     odds = [pair for pair in up_pairs(slabs) + down_pairs(slabs) if min(pair) % 2 == 1]
     swap = [(0, 1), (1, 0)]
+    weight = obs_weight.reshape(Z * Y, sensors)
     hbm = pl.BlockSpec(memory_space=pltpu.HBM)
     starts = [
         pltpu.with_memory_space_constraint(value, pltpu.HBM) for value in (u_start, crack_label)
     ]
-    to_first, to_second = call(
-        send_kernel,
-        [planes, planes],
+    moved, damage, to_first, to_second = call(
+        load_kernel,
+        [vector, field, planes, planes],
         *starts,
-        scratch=[pltpu.VMEM((2, 1, Y, X), jnp.int32), pltpu.SemaphoreType.DMA((2, 4))],
+        scratch=[pltpu.VMEM((Z, Y, X), jnp.int32), pltpu.SemaphoreType.DMA((4,))],
         in_specs=[hbm, hbm],
     )
-    moved, damage, cols = call(
-        load_kernel,
-        [vector, field, columns],
-        *starts,
-        to_first,
-        scratch=[pltpu.VMEM((Z, Y, X), jnp.int32), pltpu.SemaphoreType.DMA((4,))],
-        in_specs=[hbm, hbm, VMEM],
-    )
+    cols = call(columns_kernel, columns, moved, damage, to_first)
     for step in range(2):
         last = step == 1
         first = lax.ppermute(to_first, "slab", evens)
@@ -778,18 +761,15 @@
         )
         ys = [lax.ppermute(y, "pencil", pairs) for y, pairs in zip(out, y_pairs)]
         after = [out[0]]
-        if not last:
-            inner_rows, outer_rows = call(
-                functools.partial(weights_kernel, Z, Y),
-                [
-                    shape((2 * (Z - 4) * Y, sensors), jnp.bfloat16),
-                    shape((8 * Y, sensors), jnp.bfloat16),
-                ],
-                obs_weight.reshape(Z * Y, sensors),
+        if last:
+            picks = call(
+                functools.partial(picks_kernel, Z, Y),
+                shape((Z * Y, sensors), jnp.bfloat16),
                 sensor_cell.reshape(1, sensors),
+                weight,
                 out[0],
             )
-            after.append(inner_rows)
+            after.append(picks)
         inner_outs = margins if last else margins + [shape((Z - 2, Y, X), F32)]
         middle = call(
             functools.partial(middle_kernel, last), inner_outs, moved, damage, toughness, xh, *after
@@ -819,24 +799,22 @@
         if not last:
             inner = run_inner(corner_columns)
         U, D, S = inner[:3]
-        args = [moved, S, corner_columns]
-        outs = [shape((3, Z - 4, Y, X), F32)]
-        if last:
-            args.append(inner_rows)
-            outs.append(shape((SUB, sensors), F32))
-        inner_moved, *more = call(
+        inner_moved, *inner_sums = call(
             functools.partial(moved_kernel, last),
-            outs,
-            *args,
-            scratch=[pltpu.VMEM(((Z - 4) * Y, LANES), F32)] if last else [],
+            [shape((3, Z - 4, Y, X), F32)] + ([shape((SUB, (Z - 4) * Y), F32)] if last else []),
+            moved,
+            S,
+            corner_columns,
+            scratch=[pltpu.VMEM((3, (Z - 4) * Y, LANES), F32)] if last else [],
         )
-        if last:
-            more.append(outer_rows)
         crows = [lax.ppermute(y, "pencil", pairs) for y, pairs in zip(corner_rows, y_pairs)]
         ccols = lax.ppermute(corner_columns, "comp", swap)
-        E, *more_damage = call(
-            edge_kernel,
-            [edges] if last else [edges, shape((2, Y, X), F32)],
+        extra = shape((3, 2 * Y, LANES), F32) if last else shape((2, Y, X), F32)
+        E, near_moved, near = call(
+            functools.partial(edge_kernel, last),
+            [edges, shape((3, 2, Y, X), F32), extra],
+            moved,
+            S,
             U,
             D,
             toughness,
@@ -849,24 +827,28 @@
                 functools.partial(outer_kernel, merged, True),
                 [
                     edges,
-                    shape((3, 4, Y, X), F32),
+                    shape((3, 2, Y, X), F32),
                     shape((3, sensors // (SUB * LANES), SUB, LANES), F32),
                 ],
                 *args,
-                *more,
-                scratch=scratch + [pltpu.VMEM((4 * Y, LANES), F32)],
+                *inner_sums,
+                near,
+                weight,
+                picks,
+                scratch=scratch + [pltpu.VMEM((3, 4 * Y, LANES), F32)],
                 alias={9: 0},
             )
             damage = call(damage_kernel, field, U, D, toughness, first, second, part, micros=2)
-            moved = call(fields_kernel, vector, inner_moved, edge_moved)
+            moved = call(fields_kernel, vector, inner_moved, near_moved, edge_moved)
         else:
             _, moved, damage, cols, to_first, to_second = call(
                 functools.partial(outer_kernel, merged, False),
                 [edges, vector, field, columns, planes, planes],
                 *args,
                 inner_moved,
+                near_moved,
                 inner[3],
-                *more_damage,
+                near,
                 scratch=scratch,
                 alias={9: 0},
             )

time: 48.2 us -> 47.1 us (0.977)
  Pallas kernels: 18.2 us -> 13.7 us
  starting transfers between devices: 18.7 us -> 21.4 us
  waiting for transfers between devices: 10.3 us -> 11 us
    pallas_call x22, Pallas kernels: 18.2 us -> 13.7 us  [call(): pl.pallas_call(kernel, out_shape=outs, in_specs=in_specs or [VMEM] * len(...]
    ppermute x2, starting transfers between devices: 1.74 us -> 3.11 us  [local(): lax.ppermute(y, 'pencil', pairs)]
    ppermute x2, waiting for transfers between devices: 0.01 us -> 1.21 us  [local(): first = lax.ppermute(to_first, 'slab', evens)]
    ppermute x2, starting transfers between devices: 7.1 us -> 7.68 us  [local(): first = lax.ppermute(to_first, 'slab', evens)]
  transfers between devices with their start and end apart: 17 -> 17, of which waited for: 7 -> 9; matrix products, arithmetic and copies ran while one was open for 0% -> 0% of each run, Pallas kernels for 28% -> 20%
where the time goes in v1:
time: 47.1 us; the launch traced here: 46.9 us
  starting transfers between devices  21.4 us (45%)
  Pallas kernels  13.7 us (29%)
  waiting for transfers between devices  11 us (23%)
  between operations  0.8 us (2%)
    pallas_call x22, Pallas kernels, call(): pl.pallas_call(kernel, out_shape=outs, in_specs=in_specs or [VMEM] * len(...  13.7 us
    ppermute x2, starting transfers between devices, local(): first = lax.ppermute(to_first, 'slab', evens)  7.68 us
    ppermute x3, starting transfers between devices, all_sum(): lax.ppermute(value, 'slab', [(i, i ^ k * bit) for i in range(count)])  4.45 us
    ppermute x2, waiting for transfers between devices, all_sum(): other = lax.ppermute(value, axis, [(i, i ^ bit) for i in range(count)])  3.82 us
    ppermute x2, starting transfers between devices, local(): ys = [lax.ppermute(y, 'pencil', pairs) for y, pairs in zip(out, y_pairs)]  3.11 us
    ppermute x2, starting transfers between devices, local(): lax.ppermute(y, 'pencil', pairs)  3.11 us
    ppermute x2, waiting for transfers between devices, local(): xh = lax.ppermute(cols, 'comp', swap)  2.34 us
    ppermute x2, waiting for transfers between devices, local(): ys = [lax.ppermute(y, 'pencil', pairs) for y, pairs in zip(out, y_pairs)]  1.84 us
  transfers between devices with their start and end apart: 17, of which 9 were waited for; matrix products, arithmetic and copies ran while one was open for 0% of the time, Pallas kernels for 20%

profile of v1, /device:TPU:0, one launch (start us, length us, event | category | flops | bytes accessed | tf_op | source)
XLA Modules:
  0.0 46.9 jit_solution(7931113789980686339)
XLA Ops:
  0.6 1.3 %shard_map.76 = (f32[3,8,32,256]{3,2,1,0:T(8,128)S(1)}, f32[8,32,256]{2,1,0:T(8,128)S(1)}, f32[7,32,256]{2,1,0:T(8,128)S(1)}, f32[7,32,256]{2,1,0:T(8,128)S(1)}) custom-call(f32[3,8,32,256]{3,2,1,0:T(8,128)} %u_hbm.1, s32[8,32,256]{2,1,0:T(8,128)} %label_hbm.1), custom_call_target="tpu_custom_call" | custom-call | bytes 3000000 | tf_op jit(solution)/shard_map/pallas_call | solution.py:671
  2.0 0.7 %collective-permute-start.1 = (f32[7,32,256]{2,1,0:T(8,128)S(1)}, f32[7,32,256]{2,1,0:T(8,128)S(1)}, u32[]{:S(2)}, u32[]{:S(2)}) collective-permute-start(f32[7,32,256]{2,1,0:T(8,128)S(1)} %get-tuple-element.38), channel_id=1, source_target_pairs={{4,8},{8,4},{5,9},{9,5},{6,10},{10,6},{7,11},{11,7},{20,24},{24,20... | collective-permute-start | bytes 688136 | tf_op jit(solution)/shard_map/ppermute | solution.py:757
  2.7 5.9 %collective-permute-start = (f32[7,32,256]{2,1,0:T(8,128)S(1)}, f32[7,32,256]{2,1,0:T(8,128)S(1)}, u32[]{:S(2)}, u32[]{:S(2)}) collective-permute-start(f32[7,32,256]{2,1,0:T(8,128)S(1)} %get-tuple-element.37.first), channel_id=1, source_target_pairs={{0,4},{8,12},{4,0},{12,8},{1,5},{9,13},{5,1},{13,9},{2,6},{10,14},... | collective-permute-start | bytes 688136 | tf_op jit(solution)/shard_map/ppermute | solution.py:756
  8.9 1.2 %collective-permute-done.2.xh = f32[32,128]{1,0:T(8,128)S(1)} collective-permute-done((f32[32,128]{1,0:T(8,128)S(1)}, f32[32,128]{1,0:T(8,128)S(1)}, u32[]{:S(2)}, u32[]{:S(2)}) %collective-permute-start.2) | collective-permute-done | bytes 16416 | tf_op jit(solution)/shard_map/ppermute | solution.py:758
  10.1 1.6 %collective-permute-start.5 = (f32[8,8,256]{2,1,0:T(8,128)S(1)}, f32[8,8,256]{2,1,0:T(8,128)S(1)}, u32[]{:S(2)}, u32[]{:S(2)}) collective-permute-start(f32[8,8,256]{2,1,0:T(8,128)S(1)} %shard_map.78.rest_0_), channel_id=1, source_target_pairs={{0,2},{2,0},{1,3},{3,1},{4,6},{6,4},{5,7},{7,5},{8,10},{10,8},{9,1... | collective-permute-start | bytes 196616 | tf_op jit(solution)/shard_map/ppermute | solution.py:762
  11.7 1.0 %shard_map.79 = (f32[3,8,48,384]{3,2,1,0:T(8,128)S(1)}, f32[8,48,384]{2,1,0:T(8,128)S(1)}, f32[6,6,48,384]{3,2,1,0:T(8,128)S(1)}, f32[6,32,256]{2,1,0:T(8,128)S(1)}) custom-call(f32[3,8,32,256]{3,2,1,0:T(8,128)S(1)} %get-tuple-element.36.u.refs_0_, f32[8,32,256]{2,1,0:T(8,128)S(1)} %get-tuple-element.39.d, f32[8,32,256]{2,1,0:T(8,128)S(1)} %copy-done, ...), custom_call_target="tpu_custom_call" | custom-call | bytes 3000000 | tf_op jit(solution)/shard_map/pallas_call | solution.py:671
  12.7 1.2 %collective-permute-done.first.refs_1_ = f32[7,32,256]{2,1,0:T(8,128)S(1)} collective-permute-done((f32[7,32,256]{2,1,0:T(8,128)S(1)}, f32[7,32,256]{2,1,0:T(8,128)S(1)}, u32[]{:S(2)}, u32[]{:S(2)}) %collective-permute-start) | collective-permute-done | bytes 229408 | tf_op jit(solution)/shard_map/ppermute | solution.py:756
  14.1 1.6 %collective-permute-start.3 = (f32[8,256]{1,0:T(8,128)S(1)}, f32[8,256]{1,0:T(8,128)S(1)}, u32[]{:S(2)}, u32[]{:S(2)}) collective-permute-start(f32[8,256]{1,0:T(8,128)S(1)} %shard_map.80.after), channel_id=1, source_target_pairs={{0,2},{2,0},{1,3},{3,1},{4,6},{6,4},{5,7},{7,5},{8,10},{10,8},{9,1... | collective-permute-start | bytes 24584 | tf_op jit(solution)/shard_map/ppermute | solution.py:810
  15.7 1.0 %shard_map.82 = (f32[3,8,48,384]{3,2,1,0:T(8,128)S(1)}, f32[8,48,384]{2,1,0:T(8,128)S(1)}, f32[6,6,48,384]{3,2,1,0:T(8,128)S(1)}, f32[6,32,256]{2,1,0:T(8,128)S(1)}) custom-call(f32[8,32,256]{2,1,0:T(8,128)S(1)} %copy-done, f32[8,8,256]{2,1,0:T(8,128)S(1)} %collective-permute-done.5.ylo.yhi, ...), custom_call_target="tpu_custom_call", output_to_operand_aliasing={{0}: (4, {}), {1}: (5, {}), {2}: (6, {}), {3}: (7, {})} | custom-call | bytes 6000000 | tf_op jit(solution)/shard_map/pallas_call | solution.py:671
  17.1 0.7 %shard_map.83 = (f32[2,6,48,384]{3,2,1,0:T(8,128)S(1)}, f32[3,2,32,256]{3,2,1,0:T(8,128)S(1)}, f32[2,32,256]{2,1,0:T(8,128)S(1)}) custom-call(f32[3,8,32,256]{3,2,1,0:T(8,128)S(1)} %get-tuple-element.36.u.refs_0_, f32[6,6,48,384]{3,2,1,0:T(8,128)S(1)} %get-tuple-element.46.inner.S.refs_8_, f32[3,8,48,384]{3,2,1,0:T(8,128)S(1)} %get-tuple-element.44.U.refs_6_, ...), custom_call_target="tpu_custom_call" | custom-call | bytes 3000000 | tf_op jit(solution)/shard_map/pallas_call | solution.py:671
  17.9 0.9 %shard_map.85 = (f32[2,6,48,384]{3,2,1,0:T(8,128)S(1)}, f32[3,8,32,256]{3,2,1,0:T(8,128)S(1)}, f32[8,32,256]{2,1,0:T(8,128)S(1)}, f32[32,128]{1,0:T(8,128)S(1)},...) custom-call(f32[3,8,32,256]{3,2,1,0:T(8,128)S(1)} %get-tuple-element.36.u.refs_0_, ...), custom_call_target="tpu_custom_call", output_to_operand_aliasing={{0}: (9, {})} | custom-call | bytes 3000000 | tf_op jit(solution)/shard_map/pallas_call | solution.py:671
  18.7 1.7 %collective-permute-start.8 = (f32[7,32,256]{2,1,0:T(8,128)S(1)}, f32[7,32,256]{2,1,0:T(8,128)S(1)}, u32[]{:S(2)}, u32[]{:S(2)}) collective-permute-start(f32[7,32,256]{2,1,0:T(8,128)S(1)} %get-tuple-element.58), channel_id=1, source_target_pairs={{0,4},{8,12},{4,0},{12,8},{1,5},{9,13},{5,1},{13,9},{2,6},{10,14},... | collective-permute-start | bytes 688136 | tf_op jit(solution)/shard_map/ppermute | solution.py:756
  20.5 0.7 %collective-permute-start.9 = (f32[7,32,256]{2,1,0:T(8,128)S(1)}, f32[7,32,256]{2,1,0:T(8,128)S(1)}, u32[]{:S(2)}, u32[]{:S(2)}) collective-permute-start(f32[7,32,256]{2,1,0:T(8,128)S(1)} %get-tuple-element.59), channel_id=1, source_target_pairs={{4,8},{8,4},{5,9},{9,5},{6,10},{10,6},{7,11},{11,7},{20,24},{24,20... | collective-permute-start | bytes 688136 | tf_op jit(solution)/shard_map/ppermute | solution.py:757
  21.2 1.2 %collective-permute-done.6.xh.after = f32[32,128]{1,0:T(8,128)S(1)} collective-permute-done((f32[32,128]{1,0:T(8,128)S(1)}, f32[32,128]{1,0:T(8,128)S(1)}, u32[]{:S(2)}, u32[]{:S(2)}) %collective-permute-start.6) | collective-permute-done | bytes 16416 | tf_op jit(solution)/shard_map/ppermute | solution.py:758
  22.4 1.6 %collective-permute-start.7 = (f32[8,8,256]{2,1,0:T(8,128)S(1)}, f32[8,8,256]{2,1,0:T(8,128)S(1)}, u32[]{:S(2)}, u32[]{:S(2)}) collective-permute-start(f32[8,8,256]{2,1,0:T(8,128)S(1)} %shard_map.86.after.rest_0_), channel_id=1, source_target_pairs={{0,2},{2,0},{1,3},{3,1},{4,6},{6,4},{5,7},{7,5},{8,10},{10,8},{9,1... | collective-permute-start | bytes 196616 | tf_op jit(solution)/shard_map/ppermute | solution.py:762
  24.4 0.5 %shard_map.88 = (f32[3,8,48,384]{3,2,1,0:T(8,128)S(1)}, f32[8,48,384]{2,1,0:T(8,128)S(1)}, f32[6,6,48,384]{3,2,1,0:T(8,128)S(1)}) custom-call(f32[3,8,32,256]{3,2,1,0:T(8,128)S(1)} %get-tuple-element.51.u.refs_0_, f32[8,32,256]{2,1,0:T(8,128)S(1)} %get-tuple-element.52.d, f32[8,32,256]{2,1,0:T(8,128)S(1)} %copy-done, ...), custom_call_target="tpu_custom_call" | custom-call | bytes 3000000 | tf_op jit(solution)/shard_map/pallas_call | solution.py:671
  24.9 1.8 %collective-permute-done.7.ylo.yhi = f32[8,8,256]{2,1,0:T(8,128)S(1)} collective-permute-done((f32[8,8,256]{2,1,0:T(8,128)S(1)}, f32[8,8,256]{2,1,0:T(8,128)S(1)}, u32[]{:S(2)}, u32[]{:S(2)}) %collective-permute-start.7) | collective-permute-done | bytes 65568 | tf_op jit(solution)/shard_map/ppermute | solution.py:762
  26.8 0.6 %shard_map.89 = (f32[3,8,48,384]{3,2,1,0:T(8,128)S(1)}, f32[8,48,384]{2,1,0:T(8,128)S(1)}, f32[6,6,48,384]{3,2,1,0:T(8,128)S(1)}) custom-call(f32[8,32,256]{2,1,0:T(8,128)S(1)} %copy-done, f32[8,8,256]{2,1,0:T(8,128)S(1)} %collective-permute-done.7.ylo.yhi, ...), custom_call_target="tpu_custom_call", output_to_operand_aliasing={{0}: (4, {}), {1}: (5, {}), {2}: (6, {})} | custom-call | bytes 6000000 | tf_op jit(solution)/shard_map/pallas_call | solution.py:671
  27.6 1.6 %collective-permute-start.10 = (f32[8,256]{1,0:T(8,128)S(1)}, f32[8,256]{1,0:T(8,128)S(1)}, u32[]{:S(2)}, u32[]{:S(2)}) collective-permute-start(f32[8,256]{1,0:T(8,128)S(1)} %shard_map.90.after), channel_id=1, source_target_pairs={{0,2},{2,0},{1,3},{3,1},{4,6},{6,4},{5,7},{7,5},{8,10},{10,8},{9,1... | collective-permute-start | bytes 24584 | tf_op jit(solution)/shard_map/ppermute | solution.py:810
  29.2 0.5 shard_map.92
  29.6 0.4 shard_map.93
  30.0 1.3 %collective-permute-done.10.refs_3_.refs_4_ = f32[8,256]{1,0:T(8,128)S(1)} collective-permute-done((f32[8,256]{1,0:T(8,128)S(1)}, f32[8,256]{1,0:T(8,128)S(1)}, u32[]{:S(2)}, u32[]{:S(2)}) %collective-permute-start.10) | collective-permute-done | bytes 8224 | tf_op jit(solution)/shard_map/ppermute | solution.py:810
  31.3 1.3 %shard_map.94 = (f32[2,6,48,384]{3,2,1,0:T(8,128)S(1)}, f32[3,2,32,256]{3,2,1,0:T(8,128)S(1)}, f32[3,4,8,128]{3,2,1,0:T(8,128)S(1)}) custom-call(f32[3,8,32,256]{3,2,1,0:T(8,128)S(1)} %get-tuple-element.51.u.refs_0_, f32[7,32,256]{2,1,0:T(8,128)S(1)} %collective-permute-done.8.first.refs_1_, ...), custom_call_target="tpu_custom_call", output_to_operand_aliasing={{0}: (9, {})} | custom-call | bytes 3000000 | tf_op jit(solution)/shard_map/pallas_call | solution.py:671
  32.7 1.2 %collective-permute-done.12 = f32[3,4,8,128]{3,2,1,0:T(8,128)S(1)} collective-permute-done((f32[3,4,8,128]{3,2,1,0:T(8,128)S(1)}, f32[3,4,8,128]{3,2,1,0:T(8,128)S(1)}, u32[]{:S(2)}, u32[]{:S(2)}) %collective-permute-start.12) | collective-permute-done | bytes 49184 | tf_op jit(solution)/shard_map/ppermute | solution.py:698
  33.9 1.6 %collective-permute-start.13 = (f32[3,4,8,128]{3,2,1,0:T(8,128)S(1)}, f32[3,4,8,128]{3,2,1,0:T(8,128)S(1)}, u32[]{:S(2)}, u32[]{:S(2)}) collective-permute-start(f32[3,4,8,128]{3,2,1,0:T(8,128)S(1)} %add.6), channel_id=1, source_target_pairs={{0,2},{2,0},{1,3},{3,1},{4,6},{6,4},{5,7},{7,5},{8,10},{10,8},{9,1... | collective-permute-start | bytes 147464 | tf_op jit(solution)/shard_map/ppermute | solution.py:698
  35.4 2.6 %collective-permute-done.13 = f32[3,4,8,128]{3,2,1,0:T(8,128)S(1)} collective-permute-done((f32[3,4,8,128]{3,2,1,0:T(8,128)S(1)}, f32[3,4,8,128]{3,2,1,0:T(8,128)S(1)}, u32[]{:S(2)}, u32[]{:S(2)}) %collective-permute-start.13) | collective-permute-done | bytes 49184 | tf_op jit(solution)/shard_map/ppermute | solution.py:698
  38.1 1.4 %collective-permute-start.16 = (f32[3,4,8,128]{3,2,1,0:T(8,128)S(1)}, f32[3,4,8,128]{3,2,1,0:T(8,128)S(1)}, u32[]{:S(2)}, u32[]{:S(2)}) collective-permute-start(f32[3,4,8,128]{3,2,1,0:T(8,128)S(1)} %add.7.refs_0_), channel_id=1, source_target_pairs={{0,12},{4,8},{8,4},{12,0},{1,13},{5,9},{9,5},{13,1},{2,14},{6,10},... | collective-permute-start | bytes 147464 | tf_op jit(solution)/shard_map/ppermute | solution.py:708
  39.5 2.7 %collective-permute-start.15 = (f32[3,4,8,128]{3,2,1,0:T(8,128)S(1)}, f32[3,4,8,128]{3,2,1,0:T(8,128)S(1)}, u32[]{:S(2)}, u32[]{:S(2)}) collective-permute-start(f32[3,4,8,128]{3,2,1,0:T(8,128)S(1)} %add.7.refs_0_), channel_id=1, source_target_pairs={{0,8},{4,12},{8,0},{12,4},{1,9},{5,13},{9,1},{13,5},{2,10},{6,14},... | collective-permute-start | bytes 147464 | tf_op jit(solution)/shard_map/ppermute | solution.py:708
  42.5 0.9 %shard_map.95 = f32[3,8,32,256]{3,2,1,0:T(8,128)} custom-call(f32[3,4,32,256]{3,2,1,0:T(8,128)S(1)} %get-tuple-element.60.inner_moved, f32[3,2,32,256]{3,2,1,0:T(8,128)S(1)} %get-tuple-element.63.near_moved, f32[3,2,32,256]{3,2,1,0:T(8,128)S(1)} %get-tuple-element.67.edge_moved), custom_call_target="tpu_custom_call" | custom-call | bytes 3000000 | tf_op jit(solution)/shard_map/pallas_call | solution.py:671
  43.4 2.4 %shard_map.96 = f32[8,32,256]{2,1,0:T(8,128)} custom-call(f32[3,8,48,384]{3,2,1,0:T(8,128)S(1)} %get-tuple-element.61.U.refs_6_, f32[8,48,384]{2,1,0:T(8,128)S(1)} %get-tuple-element.62.D.refs_7_, f32[8,32,256]{2,1,0:T(8,128)S(1)} %copy-done, f32[7,32,256]{2,1,0:T(8,128)S(1)} %collective-permute-done.8.first.refs_1_, ...), custom_call_target="tpu_custom_call" | custom-call | bytes 6000000 | tf_op jit(solution)/shard_map/pallas_call | solution.py:671
  45.9 0.4 collective-permute-done.14.refs_1_
  46.3 0.7 %shard_map.97 = f32[3,4096]{1,0:T(4,128)} custom-call(f32[3,4,8,128]{3,2,1,0:T(8,128)S(1)} %add.7.refs_0_, f32[3,4,8,128]{3,2,1,0:T(8,128)S(1)} %collective-permute-done.14.refs_1_, f32[3,4,8,128]{3,2,1,0:T(8,128)S(1)} %collective-permute-done.15.refs_2_, f32[3,4,8,128]{3,2,1,0:T(8,128)S(1)} %collective-permute-done.16.refs_3_), custom_call_target="tpu_custom_call" | custom-call | bytes 3000000 | tf_op jit(solution)/shard_map/pallas_call | solution.py:671
  (32 shorter events, 2.1 us)
Async XLA Ops:
  0.6 11.0 %copy-start = (f32[8,32,256]{2,1,0:T(8,128)S(1)}, f32[8,32,256]{2,1,0:T(8,128)}, u32[]{:S(2)}) copy-start(f32[8,32,256]{2,1,0:T(8,128)} %tough.13) | copy-start | bytes 786436
  2.0 10.7 %collective-permute-start.1 = (f32[7,32,256]{2,1,0:T(8,128)S(1)}, f32[7,32,256]{2,1,0:T(8,128)S(1)}, u32[]{:S(2)}, u32[]{:S(2)}) collective-permute-start(f32[7,32,256]{2,1,0:T(8,128)S(1)} %get-tuple-element.38), channel_id=1, source_target_pairs={{4,8},{8,4},{5,9},{9,5},{6,10},{10,6},{7,11},{11,7},{20,24},{24,20... | collective-permute-start | bytes 688136 | tf_op jit(solution)/shard_map/ppermute | solution.py:757
  2.7 11.3 %collective-permute-start = (f32[7,32,256]{2,1,0:T(8,128)S(1)}, f32[7,32,256]{2,1,0:T(8,128)S(1)}, u32[]{:S(2)}, u32[]{:S(2)}) collective-permute-start(f32[7,32,256]{2,1,0:T(8,128)S(1)} %get-tuple-element.37.first), channel_id=1, source_target_pairs={{0,4},{8,12},{4,0},{12,8},{1,5},{9,13},{5,1},{13,9},{2,6},{10,14},... | collective-permute-start | bytes 688136 | tf_op jit(solution)/shard_map/ppermute | solution.py:756
  8.9 1.2 %collective-permute-start.2 = (f32[32,128]{1,0:T(8,128)S(1)}, f32[32,128]{1,0:T(8,128)S(1)}, u32[]{:S(2)}, u32[]{:S(2)}) collective-permute-start(f32[32,128]{1,0:T(8,128)S(1)} %shard_map.77), channel_id=1, source_target_pairs={{0,1},{1,0},{2,3},{3,2},{4,5},{5,4},{6,7},{7,6},{8,9},{9,8},{10,11... | collective-permute-start | bytes 49160 | tf_op jit(solution)/shard_map/ppermute | solution.py:758
  10.1 5.6 %collective-permute-start.5 = (f32[8,8,256]{2,1,0:T(8,128)S(1)}, f32[8,8,256]{2,1,0:T(8,128)S(1)}, u32[]{:S(2)}, u32[]{:S(2)}) collective-permute-start(f32[8,8,256]{2,1,0:T(8,128)S(1)} %shard_map.78.rest_0_), channel_id=1, source_target_pairs={{0,2},{2,0},{1,3},{3,1},{4,6},{6,4},{5,7},{7,5},{8,10},{10,8},{9,1... | collective-permute-start | bytes 196616 | tf_op jit(solution)/shard_map/ppermute | solution.py:762
  14.1 3.7 %collective-permute-start.4 = (f32[32,128]{1,0:T(8,128)S(1)}, f32[32,128]{1,0:T(8,128)S(1)}, u32[]{:S(2)}, u32[]{:S(2)}) collective-permute-start(f32[32,128]{1,0:T(8,128)S(1)} %shard_map.81.after), channel_id=1, source_target_pairs={{0,1},{1,0},{2,3},{3,2},{4,5},{5,4},{6,7},{7,6},{8,9},{9,8},{10,11... | collective-permute-start | bytes 49160 | tf_op jit(solution)/shard_map/ppermute | solution.py:811
  14.1 3.7 %collective-permute-start.3 = (f32[8,256]{1,0:T(8,128)S(1)}, f32[8,256]{1,0:T(8,128)S(1)}, u32[]{:S(2)}, u32[]{:S(2)}) collective-permute-start(f32[8,256]{1,0:T(8,128)S(1)} %shard_map.80.after), channel_id=1, source_target_pairs={{0,2},{2,0},{1,3},{3,1},{4,6},{6,4},{5,7},{7,5},{8,10},{10,8},{9,1... | collective-permute-start | bytes 24584 | tf_op jit(solution)/shard_map/ppermute | solution.py:810
  17.9 6.1 %copy-start.1 = (bf16[8,32,1,4096]{3,1,2,0:T(8,128)(2,1)S(1)}, bf16[8,32,1,4096]{3,1,2,0:T(8,128)(2,1)}, u32[]{:S(2)}) copy-start(bf16[8,32,1,4096]{3,1,2,0:T(8,128)(2,1)} %param.8) | copy-start | bytes 6291460
  17.9 6.1 %copy-start.2 = (s32[4096]{0:T(1024)S(1)}, s32[4096]{0:T(1024)}, u32[]{:S(2)}) copy-start(s32[4096]{0:T(1024)} %param.9) | copy-start | bytes 49156
  18.7 8.6 %collective-permute-start.8 = (f32[7,32,256]{2,1,0:T(8,128)S(1)}, f32[7,32,256]{2,1,0:T(8,128)S(1)}, u32[]{:S(2)}, u32[]{:S(2)}) collective-permute-start(f32[7,32,256]{2,1,0:T(8,128)S(1)} %get-tuple-element.58), channel_id=1, source_target_pairs={{0,4},{8,12},{4,0},{12,8},{1,5},{9,13},{5,1},{13,9},{2,6},{10,14},... | collective-permute-start | bytes 688136 | tf_op jit(solution)/shard_map/ppermute | solution.py:756
  20.5 6.9 %collective-permute-start.9 = (f32[7,32,256]{2,1,0:T(8,128)S(1)}, f32[7,32,256]{2,1,0:T(8,128)S(1)}, u32[]{:S(2)}, u32[]{:S(2)}) collective-permute-start(f32[7,32,256]{2,1,0:T(8,128)S(1)} %get-tuple-element.59), channel_id=1, source_target_pairs={{4,8},{8,4},{5,9},{9,5},{6,10},{10,6},{7,11},{11,7},{20,24},{24,20... | collective-permute-start | bytes 688136 | tf_op jit(solution)/shard_map/ppermute | solution.py:757
  21.1 1.2 %collective-permute-start.6 = (f32[32,128]{1,0:T(8,128)S(1)}, f32[32,128]{1,0:T(8,128)S(1)}, u32[]{:S(2)}, u32[]{:S(2)}) collective-permute-start(f32[32,128]{1,0:T(8,128)S(1)} %get-tuple-element.53), channel_id=1, source_target_pairs={{0,1},{1,0},{2,3},{3,2},{4,5},{5,4},{6,7},{7,6},{8,9},{9,8},{10,11... | collective-permute-start | bytes 49160 | tf_op jit(solution)/shard_map/ppermute | solution.py:758
  22.4 4.3 %collective-permute-start.7 = (f32[8,8,256]{2,1,0:T(8,128)S(1)}, f32[8,8,256]{2,1,0:T(8,128)S(1)}, u32[]{:S(2)}, u32[]{:S(2)}) collective-permute-start(f32[8,8,256]{2,1,0:T(8,128)S(1)} %shard_map.86.after.rest_0_), channel_id=1, source_target_pairs={{0,2},{2,0},{1,3},{3,1},{4,6},{6,4},{5,7},{7,5},{8,10},{10,8},{9,1... | collective-permute-start | bytes 196616 | tf_op jit(solution)/shard_map/ppermute | solution.py:762
  27.6 3.7 %collective-permute-start.11 = (f32[32,128]{1,0:T(8,128)S(1)}, f32[32,128]{1,0:T(8,128)S(1)}, u32[]{:S(2)}, u32[]{:S(2)}) collective-permute-start(f32[32,128]{1,0:T(8,128)S(1)} %shard_map.91.after), channel_id=1, source_target_pairs={{0,1},{1,0},{2,3},{3,2},{4,5},{5,4},{6,7},{7,6},{8,9},{9,8},{10,11... | collective-permute-start | bytes 49160 | tf_op jit(solution)/shard_map/ppermute | solution.py:811
  27.6 3.7 %collective-permute-start.10 = (f32[8,256]{1,0:T(8,128)S(1)}, f32[8,256]{1,0:T(8,128)S(1)}, u32[]{:S(2)}, u32[]{:S(2)}) collective-permute-start(f32[8,256]{1,0:T(8,128)S(1)} %shard_map.90.after), channel_id=1, source_target_pairs={{0,2},{2,0},{1,3},{3,1},{4,6},{6,4},{5,7},{7,5},{8,10},{10,8},{9,1... | collective-permute-start | bytes 24584 | tf_op jit(solution)/shard_map/ppermute | solution.py:810
  32.6 1.3 %collective-permute-start.12 = (f32[3,4,8,128]{3,2,1,0:T(8,128)S(1)}, f32[3,4,8,128]{3,2,1,0:T(8,128)S(1)}, u32[]{:S(2)}, u32[]{:S(2)}) collective-permute-start(f32[3,4,8,128]{3,2,1,0:T(8,128)S(1)} %get-tuple-element.68.after), channel_id=1, source_target_pairs={{0,1},{1,0},{2,3},{3,2},{4,5},{5,4},{6,7},{7,6},{8,9},{9,8},{10,11... | collective-permute-start | bytes 147464 | tf_op jit(solution)/shard_map/ppermute | solution.py:698
  33.9 4.2 %collective-permute-start.13 = (f32[3,4,8,128]{3,2,1,0:T(8,128)S(1)}, f32[3,4,8,128]{3,2,1,0:T(8,128)S(1)}, u32[]{:S(2)}, u32[]{:S(2)}) collective-permute-start(f32[3,4,8,128]{3,2,1,0:T(8,128)S(1)} %add.6), channel_id=1, source_target_pairs={{0,2},{2,0},{1,3},{3,1},{4,6},{6,4},{5,7},{7,5},{8,10},{10,8},{9,1... | collective-permute-start | bytes 147464 | tf_op jit(solution)/shard_map/ppermute | solution.py:698
  38.1 7.8 %collective-permute-start.16 = (f32[3,4,8,128]{3,2,1,0:T(8,128)S(1)}, f32[3,4,8,128]{3,2,1,0:T(8,128)S(1)}, u32[]{:S(2)}, u32[]{:S(2)}) collective-permute-start(f32[3,4,8,128]{3,2,1,0:T(8,128)S(1)} %add.7.refs_0_), channel_id=1, source_target_pairs={{0,12},{4,8},{8,4},{12,0},{1,13},{5,9},{9,5},{13,1},{2,14},{6,10},... | collective-permute-start | bytes 147464 | tf_op jit(solution)/shard_map/ppermute | solution.py:708
  39.5 6.4 %collective-permute-start.15 = (f32[3,4,8,128]{3,2,1,0:T(8,128)S(1)}, f32[3,4,8,128]{3,2,1,0:T(8,128)S(1)}, u32[]{:S(2)}, u32[]{:S(2)}) collective-permute-start(f32[3,4,8,128]{3,2,1,0:T(8,128)S(1)} %add.7.refs_0_), channel_id=1, source_target_pairs={{0,8},{4,12},{8,0},{12,4},{1,9},{5,13},{9,1},{13,5},{2,10},{6,14},... | collective-permute-start | bytes 147464 | tf_op jit(solution)/shard_map/ppermute | solution.py:708
  42.2 4.1 %collective-permute-start.14 = (f32[3,4,8,128]{3,2,1,0:T(8,128)S(1)}, f32[3,4,8,128]{3,2,1,0:T(8,128)S(1)}, u32[]{:S(2)}, u32[]{:S(2)}) collective-permute-start(f32[3,4,8,128]{3,2,1,0:T(8,128)S(1)} %add.7.refs_0_), channel_id=1, source_target_pairs={{0,4},{4,0},{8,12},{12,8},{1,5},{5,1},{9,13},{13,9},{2,6},{6,2},{1... | collective-permute-start | bytes 147464 | tf_op jit(solution)/shard_map/ppermute | solution.py:708

commit v2 on v1

--- a/solution.py
+++ b/solution.py
@@ -229,15 +229,22 @@
         D[z, H + Y : H + Y + 1, 0:X] = high[z : z + 1]
 
 
-def lay_out_face(merged, k, far, near, low_rows, high_rows, columns, F):
+def lay_out_face(k, far, near, columns, F):
     Y, X = near(0).shape
     H = SUB
-    low_of, high_of = row_keepers(merged)
     column = column_reader(columns[...])
     for c in range(3):
         F[c, 0, H : H + Y, 0:X] = far(c)
         F[c, 1, H : H + Y, 0:X] = near(c)
         F[c, 1, H : H + Y, X : X + LANES] = column(3 * k + c)
+
+
+def lay_out_face_rows(merged, k, low_rows, high_rows, F):
+    X = low_rows.shape[1]
+    H = SUB
+    Y = F.shape[2] - 2 * SUB
+    low_of, high_of = row_keepers(merged)
+    for c in range(3):
         row = 3 * k + c
         F[c, 1, H - 1 : H, 0:X] = low_of(low_rows[row : row + 1, :])
         F[c, 1, H + Y : H + Y + 1, 0:X] = high_of(high_rows[row : row + 1, :])
@@ -327,8 +334,8 @@
     return gz, gy, gx
 
 
-def side_stress(at, damage_plane, S, Y, X):
-    for t in range(1, Y // SUB + 1):
+def side_stress(at, damage_plane, S, tiles, X):
+    for t in tiles:
         r = t * SUB
         rows, out = slice(r, r + SUB), slice(X, X + LANES)
         gz, gy, gx = [], [], []
@@ -345,8 +352,8 @@
         S[XX, rows, out] = h * (total + 2.0 * gx[2])
 
 
-def face_stress(at, damage, S, Y, X):
-    for t in range(1, Y // SUB + 1):
+def face_stress(at, damage, S, tiles, X):
+    for t in tiles:
         rows = slice(t * SUB, t * SUB + SUB)
         gz, gy, gx = gradients(at, t * SUB, SUB)
         h = stiffness(damage(slice((t - 1) * SUB, t * SUB)))
@@ -553,29 +560,8 @@
             )
 
 
-def outer_kernel(merged, last, *refs):
-    rest = list(refs)
-    take = lambda k: [rest.pop(0) for _ in range(k)]
-    u, first, second, low_rows, high_rows, columns, U, D, S, E_in = take(10)
-    if last:
-        inner_sums, near_pool, weight, picks = take(4)
-        E, moved, part = take(3)
-    else:
-        inner_moved, near_moved, inner_damage, edge_damage = take(4)
-        E, moved, damage, cols, to_first, to_second = take(6)
-    del E_in
-    low_face, high_face, faces = take(3)
-    if last:
-        (pool,) = take(1)
-    _, Z, Y, X = u.shape
-    tiles = range(1, Y // SUB + 1)
-    low, high = plane_readers(first, second)
-    lay_out_face(
-        merged, 0, lambda c: low(2 * c), lambda c: low(2 * c + 1), low_rows, high_rows, columns, low_face
-    )
-    lay_out_face(
-        merged, 1, lambda c: high(2 * c + 1), lambda c: high(2 * c), low_rows, high_rows, columns, high_face
-    )
+def face_planes(low_face, high_face, U):
+    Z = U.shape[1]
 
     def at_plane(z):
         def at(c, dz):
@@ -588,33 +574,80 @@
 
         return at
 
-    face_stress(at_plane(-1), lambda own: low(6, own), faces.at[0], Y, X)
-    face_stress(at_plane(Z), lambda own: high(6, own), faces.at[1], Y, X)
+    return at_plane
+
+
+def face_tiles(tiles, u, first, second, U, D, S, E, low_face, high_face, faces, put):
+    _, Z, _, X = u.shape
+    low, high = plane_readers(first, second)
+    at_plane = face_planes(low_face, high_face, U)
+    face_stress(at_plane(-1), lambda own: low(6, own), faces.at[0], tiles, X)
+    face_stress(at_plane(Z), lambda own: high(6, own), faces.at[1], tiles, X)
+    for k, z in enumerate((0, Z - 1)):
+        side_stress(at_plane(z), D.at[z], E.at[k], tiles, X)
+    around = (
+        (0, faces.at[0], E.at[0], S.at[0]),
+        (Z - 1, S.at[Z - 3], E.at[1], faces.at[1]),
+    )
+    for k, (z, below, mid, above) in enumerate(around):
+        for t in tiles:
+            put(k, t, plane_moved(below, mid, above, lambda c: u.at[c, z], t, X))
+
+
+def mid_kernel(last, u, first, second, columns, U, D, S, E_in, E, low_face, high_face, faces, *rest):
+    del E_in
+    moved, *pool = rest
+    Y = u.shape[2]
+    low, high = plane_readers(first, second)
+    lay_out_face(0, lambda c: low(2 * c), lambda c: low(2 * c + 1), columns, low_face)
+    lay_out_face(1, lambda c: high(2 * c + 1), lambda c: high(2 * c), columns, high_face)
+
+    def put(k, t, new):
+        for c in range(3):
+            moved[c, k, (t - 2) * SUB : (t - 1) * SUB, :] = new[c]
+        if last:
+            put_folded(pool[0], k * (Y - 2 * SUB) + (t - 2) * SUB, new)
+
+    tiles = range(2, Y // SUB)
+    face_tiles(tiles, u, first, second, U, D, S, E, low_face, high_face, faces, put)
+
+
+def outer_kernel(merged, last, *refs):
+    rest = list(refs)
+    take = lambda k: [rest.pop(0) for _ in range(k)]
+    u, first, second, low_rows, high_rows, U, D, S = take(8)
+    take(4)
+    if last:
+        inner_sums, near_pool, mid_pool, weight, picks = take(5)
+        E, low_face, high_face, faces, moved, part, pool = take(7)
+    else:
+        inner_moved, near_moved, mid_moved, inner_damage, near_damage = take(5)
+        E, low_face, high_face, faces, moved, damage, cols, to_first, to_second = take(9)
+    _, Z, Y, X = u.shape
+    count = Y // SUB
+    lay_out_face_rows(merged, 0, low_rows, high_rows, low_face)
+    lay_out_face_rows(merged, 1, low_rows, high_rows, high_face)
+    at_plane = face_planes(low_face, high_face, U)
     for k, z in enumerate((0, Z - 1)):
         row_stress(at_plane(z), D.at[z], E.at[k], Y, X)
-        side_stress(at_plane(z), D.at[z], E.at[k], Y, X)
-
-    def stress(z):
-        if z < 0:
-            return faces.at[0]
-        if z >= Z:
-            return faces.at[1]
-        if z == 0:
-            return E.at[0]
-        if z == Z - 1:
-            return E.at[1]
-        return S.at[z - 1]
-
-    for k, z in enumerate((0, Z - 1)):
-        for t in tiles:
-            own = slice((t - 1) * SUB, t * SUB)
-            new = plane_moved(stress(z - 1), stress(z), stress(z + 1), lambda c: u.at[c, z], t, X)
-            for c in range(3):
-                moved[c, k if last else z, own, :] = new[c]
+
+    def put(k, t, new):
+        own = slice((t - 1) * SUB, t * SUB)
+        for c in range(3):
             if last:
-                put_folded(pool, 3 * k * Y + (t - 1) * SUB, new)
+                end = 0 if t == 1 else SUB
+                moved[c, k, end : end + SUB, :] = new[c]
+            else:
+                moved[c, k * (Z - 1), own, :] = new[c]
+        if last:
+            put_folded(pool, 3 * k * Y + (t - 1) * SUB, new)
+
+    face_tiles((1, count), u, first, second, U, D, S, E, low_face, high_face, faces, put)
+    middle = Y - 2 * SUB
     if last:
+        pool[:, SUB : SUB + middle, :] = mid_pool[:, 0:middle, :]
         pool[:, Y : 3 * Y, :] = near_pool[...]
+        pool[:, 3 * Y + SUB : 3 * Y + SUB + middle, :] = mid_pool[:, middle : 2 * middle, :]
         outer_sums = sums_of(pool)
         means = jnp.concatenate(
             [outer_sums[:, 0 : 2 * Y], inner_sums[...], outer_sums[:, 2 * Y : 4 * Y]], axis=1
@@ -634,24 +667,28 @@
                 part[c, k] = tile
     else:
         for c in range(3):
+            for k in range(2):
+                moved[c, k * (Z - 1), SUB : SUB + middle, :] = mid_moved[c, k]
             moved[c, 1] = near_moved[c, 0]
             moved[c, 2 : Z - 2] = inner_moved[c]
             moved[c, Z - 2] = near_moved[c, 1]
-        damage[0] = edge_damage[0]
+        damage[0] = near_damage[0]
         damage[1 : Z - 1] = inner_damage[...]
-        damage[Z - 1] = edge_damage[1]
+        damage[Z - 1] = near_damage[1]
         put_planes(moved, damage, to_first, to_second)
         put_columns(moved, damage, cols)
 
 
-def fields_kernel(inner_moved, near_moved, edge_moved, moved):
-    Z = moved.shape[1]
-    for c in range(3):
-        moved[c, 0] = edge_moved[c, 0]
+def fields_kernel(inner_moved, near_moved, mid_moved, edge_moved, moved):
+    _, Z, Y, _ = moved.shape
+    for c in range(3):
+        for k, z in enumerate((0, Z - 1)):
+            moved[c, z, 0:SUB, :] = edge_moved[c, k, 0:SUB, :]
+            moved[c, z, SUB : Y - SUB, :] = mid_moved[c, k]
+            moved[c, z, Y - SUB : Y, :] = edge_moved[c, k, SUB : 2 * SUB, :]
         moved[c, 1] = near_moved[c, 0]
         moved[c, 2 : Z - 2] = inner_moved[c]
         moved[c, Z - 2] = near_moved[c, 1]
-        moved[c, Z - 1] = edge_moved[c, 1]
 
 
 def finish_kernel(*refs):
@@ -712,7 +749,7 @@
 def local(u_start, toughness, crack_label, obs_weight, sensor_cell):
     Z, Y, X = toughness.shape
     slabs, pencils = lax.axis_size("slab"), lax.axis_size("pencil")
-    if lax.axis_size("comp") != 2 or Z < 6 or Z % SUB or 8 * Z > LANES:
+    if lax.axis_size("comp") != 2 or Z < 6 or Z % SUB or 8 * Z > LANES or Y < 3 * SUB:
         raise ValueError("unsupported block")
     merged = pencils == 2
     n = 1 if merged else 2
@@ -728,11 +765,7 @@
         shape((Z, rows, lanes), F32),
         shape((Z - 2, 6, rows, lanes), F32),
     ]
-    scratch = [
-        pltpu.VMEM((3, 2, rows, lanes), F32),
-        pltpu.VMEM((3, 2, rows, lanes), F32),
-        pltpu.VMEM((2, 3, rows, lanes), F32),
-    ]
+    face_fields = [shape((3, 2, rows, lanes), F32)] * 2 + [shape((2, 3, rows, lanes), F32)]
     edges = shape((2, 6, rows, lanes), F32)
     planes = shape((7, Y, X), F32)
     evens = [pair for pair in up_pairs(slabs) + down_pairs(slabs) if min(pair) % 2 == 0]
@@ -786,18 +819,15 @@
                 alias={len(args) + k: k for k in range(len(inner_outs))},
             )
 
-        if last:
-            inner = run_inner(xh)
         corner_rows = call(
             functools.partial(corner_rows_kernel, merged),
             [shape((SUB, X), F32)] * n,
             first,
             second,
-            inner[2] if last else middle[2],
+            middle[2],
         )
         corner_columns = call(corner_columns_kernel, columns, first, second, corner_rows[0])
-        if not last:
-            inner = run_inner(corner_columns)
+        inner = run_inner(corner_columns)
         U, D, S = inner[:3]
         inner_moved, *inner_sums = call(
             functools.partial(moved_kernel, last),
@@ -821,36 +851,57 @@
             first,
             second,
         )
-        args = [moved, first, second, crows[0], crows[-1], ccols, U, D, S, E]
+        middle_rows = Y - 2 * SUB
+        E, low_face, high_face, faces, mid_moved, *mid_pool = call(
+            functools.partial(mid_kernel, last),
+            [edges, *face_fields, shape((3, 2, middle_rows, X), F32)]
+            + ([shape((3, 2 * middle_rows, LANES), F32)] if last else []),
+            moved,
+            first,
+            second,
+            ccols,
+            U,
+            D,
+            S,
+            E,
+            alias={7: 0},
+        )
+        args = [moved, first, second, crows[0], crows[-1], U, D, S]
+        laid = [E, low_face, high_face, faces]
+        laid_alias = {len(args) + k: k for k in range(4)}
         if last:
-            _, edge_moved, part = call(
+            *_, edge_moved, part = call(
                 functools.partial(outer_kernel, merged, True),
                 [
                     edges,
-                    shape((3, 2, Y, X), F32),
+                    *face_fields,
+                    shape((3, 2, 2 * SUB, X), F32),
                     shape((3, sensors // (SUB * LANES), SUB, LANES), F32),
                 ],
                 *args,
+                *laid,
                 *inner_sums,
                 near,
+                *mid_pool,
                 weight,
                 picks,
-                scratch=scratch + [pltpu.VMEM((3, 4 * Y, LANES), F32)],
-                alias={9: 0},
+                scratch=[pltpu.VMEM((3, 4 * Y, LANES), F32)],
+                alias=laid_alias,
             )
             damage = call(damage_kernel, field, U, D, toughness, first, second, part, micros=2)
-            moved = call(fields_kernel, vector, inner_moved, near_moved, edge_moved)
+            moved = call(fields_kernel, vector, inner_moved, near_moved, mid_moved, edge_moved)
         else:
-            _, moved, damage, cols, to_first, to_second = call(
+            *_, moved, damage, cols, to_first, to_second = call(
                 functools.partial(outer_kernel, merged, False),
-                [edges, vector, field, columns, planes, planes],
+                [edges, *face_fields, vector, field, columns, planes, planes],
                 *args,
+                *laid,
                 inner_moved,
                 near_moved,
+                mid_moved,
                 inner[3],
                 near,
-                scratch=scratch,
-                alias={9: 0},
+                alias=laid_alias,
             )
     terms = all_sum(part)
     readings = call(finish_kernel, shape((3, sensors), F32), *terms)

time: 47.1 us -> 48.4 us (1.028)
  waiting for transfers between devices: 11 us -> 12.2 us
    ppermute x3, starting transfers between devices: 4.45 us -> 6.34 us  [all_sum(): lax.ppermute(value, 'slab', [(i, i ^ k * bit) for i in range(count)])]
    ppermute x2, waiting for transfers between devices: 1.84 us -> 0.01 us  [local(): ys = [lax.ppermute(y, 'pencil', pairs) for y, pairs in zip(out, y_pairs)]]
    ppermute x2, waiting for transfers between devices: 1.21 us -> 2.6 us  [local(): first = lax.ppermute(to_first, 'slab', evens)]
    ppermute x2, waiting for transfers between devices: 3.82 us -> 4.77 us  [all_sum(): other = lax.ppermute(value, axis, [(i, i ^ bit) for i in range(count)])]
    ppermute x2, starting transfers between devices: 1.61 us -> 0.65 us  [all_sum(): other = lax.ppermute(value, axis, [(i, i ^ bit) for i in range(count)])]
    ppermute x2, starting transfers between devices: 3.11 us -> 2.32 us  [local(): lax.ppermute(y, 'pencil', pairs)]
    ppermute x3, waiting for transfers between devices: 0.43 us -> 1.22 us  [all_sum(): lax.ppermute(value, 'slab', [(i, i ^ k * bit) for i in range(count)])]
    pallas_call x22 -> x24, Pallas kernels: 13.7 us -> 13.9 us  [call(): pl.pallas_call(kernel, out_shape=outs, in_specs=in_specs or [VMEM] * len(...]
  transfers between devices with their start and end apart: 17 -> 17, of which waited for: 9 -> 8; matrix products, arithmetic and copies ran while one was open for 0% -> 0% of each run, Pallas kernels for 20% -> 21%
where the time goes in v2:
time: 48.4 us; the launch traced here: 48.3 us
  starting transfers between devices  21.2 us (44%)
  Pallas kernels  13.9 us (29%)
  waiting for transfers between devices  12.2 us (25%)
  between operations  0.84 us (2%)
    pallas_call x24, Pallas kernels, call(): pl.pallas_call(kernel, out_shape=outs, in_specs=in_specs or [VMEM] * len(...  13.9 us
    ppermute x2, starting transfers between devices, local(): first = lax.ppermute(to_first, 'slab', evens)  7.71 us
    ppermute x3, starting transfers between devices, all_sum(): lax.ppermute(value, 'slab', [(i, i ^ k * bit) for i in range(count)])  6.34 us
    ppermute x2, waiting for transfers between devices, all_sum(): other = lax.ppermute(value, axis, [(i, i ^ bit) for i in range(count)])  4.77 us
    ppermute x2, starting transfers between devices, local(): ys = [lax.ppermute(y, 'pencil', pairs) for y, pairs in zip(out, y_pairs)]  2.79 us
    ppermute x2, waiting for transfers between devices, local(): first = lax.ppermute(to_first, 'slab', evens)  2.6 us
    ppermute x2, waiting for transfers between devices, local(): xh = lax.ppermute(cols, 'comp', swap)  2.34 us
    ppermute x2, starting transfers between devices, local(): lax.ppermute(y, 'pencil', pairs)  2.32 us
  transfers between devices with their start and end apart: 17, of which 8 were waited for; matrix products, arithmetic and copies ran while one was open for 0% of the time, Pallas kernels for 21%

profile of v2, /device:TPU:0, one launch (start us, length us, event | category | flops | bytes accessed | tf_op | source)
XLA Modules:
  0.0 48.3 jit_solution(4881297253970012672)
XLA Ops:
  0.6 1.3 %shard_map.76 = (f32[3,8,32,256]{3,2,1,0:T(8,128)S(1)}, f32[8,32,256]{2,1,0:T(8,128)S(1)}, f32[7,32,256]{2,1,0:T(8,128)S(1)}, f32[7,32,256]{2,1,0:T(8,128)S(1)}) custom-call(f32[3,8,32,256]{3,2,1,0:T(8,128)} %u_hbm.1, s32[8,32,256]{2,1,0:T(8,128)} %label_hbm.1), custom_call_target="tpu_custom_call" | custom-call | bytes 3000000 | tf_op jit(solution)/shard_map/pallas_call | solution.py:708
  2.0 3.1 %collective-permute-start = (f32[7,32,256]{2,1,0:T(8,128)S(1)}, f32[7,32,256]{2,1,0:T(8,128)S(1)}, u32[]{:S(2)}, u32[]{:S(2)}) collective-permute-start(f32[7,32,256]{2,1,0:T(8,128)S(1)} %get-tuple-element.48.first), channel_id=1, source_target_pairs={{0,4},{8,12},{4,0},{12,8},{1,5},{9,13},{5,1},{13,9},{2,6},{10,14},... | collective-permute-start | bytes 688136 | tf_op jit(solution)/shard_map/ppermute | solution.py:789
  5.1 0.7 %collective-permute-start.1 = (f32[7,32,256]{2,1,0:T(8,128)S(1)}, f32[7,32,256]{2,1,0:T(8,128)S(1)}, u32[]{:S(2)}, u32[]{:S(2)}) collective-permute-start(f32[7,32,256]{2,1,0:T(8,128)S(1)} %get-tuple-element.49), channel_id=1, source_target_pairs={{4,8},{8,4},{5,9},{9,5},{6,10},{10,6},{7,11},{11,7},{20,24},{24,20... | collective-permute-start | bytes 688136 | tf_op jit(solution)/shard_map/ppermute | solution.py:790
  6.1 1.2 %collective-permute-done.2.xh = f32[32,128]{1,0:T(8,128)S(1)} collective-permute-done((f32[32,128]{1,0:T(8,128)S(1)}, f32[32,128]{1,0:T(8,128)S(1)}, u32[]{:S(2)}, u32[]{:S(2)}) %collective-permute-start.2) | collective-permute-done | bytes 16416 | tf_op jit(solution)/shard_map/ppermute | solution.py:791
  7.3 1.6 %collective-permute-start.4 = (f32[8,8,256]{2,1,0:T(8,128)S(1)}, f32[8,8,256]{2,1,0:T(8,128)S(1)}, u32[]{:S(2)}, u32[]{:S(2)}) collective-permute-start(f32[8,8,256]{2,1,0:T(8,128)S(1)} %shard_map.78.rest_0_), channel_id=1, source_target_pairs={{0,2},{2,0},{1,3},{3,1},{4,6},{6,4},{5,7},{7,5},{8,10},{10,8},{9,1... | collective-permute-start | bytes 196616 | tf_op jit(solution)/shard_map/ppermute | solution.py:795
  8.8 1.0 %shard_map.79 = (f32[3,8,48,384]{3,2,1,0:T(8,128)S(1)}, f32[8,48,384]{2,1,0:T(8,128)S(1)}, f32[6,6,48,384]{3,2,1,0:T(8,128)S(1)}, f32[6,32,256]{2,1,0:T(8,128)S(1)}) custom-call(f32[3,8,32,256]{3,2,1,0:T(8,128)S(1)} %get-tuple-element.47.u.refs_0_, f32[8,32,256]{2,1,0:T(8,128)S(1)} %get-tuple-element.50.d, f32[8,32,256]{2,1,0:T(8,128)S(1)} %copy-done, ...), custom_call_target="tpu_custom_call" | custom-call | bytes 3000000 | tf_op jit(solution)/shard_map/pallas_call | solution.py:708
  9.9 0.8 %collective-permute-done.first.refs_1_ = f32[7,32,256]{2,1,0:T(8,128)S(1)} collective-permute-done((f32[7,32,256]{2,1,0:T(8,128)S(1)}, f32[7,32,256]{2,1,0:T(8,128)S(1)}, u32[]{:S(2)}, u32[]{:S(2)}) %collective-permute-start) | collective-permute-done | bytes 229408 | tf_op jit(solution)/shard_map/ppermute | solution.py:789
  10.9 1.7 %collective-permute-start.3 = (f32[8,256]{1,0:T(8,128)S(1)}, f32[8,256]{1,0:T(8,128)S(1)}, u32[]{:S(2)}, u32[]{:S(2)}) collective-permute-start(f32[8,256]{1,0:T(8,128)S(1)} %shard_map.80.after), channel_id=1, source_target_pairs={{0,2},{2,0},{1,3},{3,1},{4,6},{6,4},{5,7},{7,5},{8,10},{10,8},{9,1... | collective-permute-start | bytes 24584 | tf_op jit(solution)/shard_map/ppermute | solution.py:840
  12.7 1.0 %shard_map.82 = (f32[3,8,48,384]{3,2,1,0:T(8,128)S(1)}, f32[8,48,384]{2,1,0:T(8,128)S(1)}, f32[6,6,48,384]{3,2,1,0:T(8,128)S(1)}, f32[6,32,256]{2,1,0:T(8,128)S(1)}) custom-call(f32[8,32,256]{2,1,0:T(8,128)S(1)} %copy-done, f32[8,8,256]{2,1,0:T(8,128)S(1)} %collective-permute-done.4.ylo.yhi, ...), custom_call_target="tpu_custom_call", output_to_operand_aliasing={{0}: (4, {}), {1}: (5, {}), {2}: (6, {}), {3}: (7, {})} | custom-call | bytes 6000000 | tf_op jit(solution)/shard_map/pallas_call | solution.py:708
  14.1 0.7 %shard_map.83 = (f32[2,6,48,384]{3,2,1,0:T(8,128)S(1)}, f32[3,2,32,256]{3,2,1,0:T(8,128)S(1)}, f32[2,32,256]{2,1,0:T(8,128)S(1)}) custom-call(f32[3,8,32,256]{3,2,1,0:T(8,128)S(1)} %get-tuple-element.47.u.refs_0_, f32[6,6,48,384]{3,2,1,0:T(8,128)S(1)} %get-tuple-element.57.inner.S.refs_7_, f32[3,8,48,384]{3,2,1,0:T(8,128)S(1)} %get-tuple-element.55.U.refs_5_, ...), custom_call_target="tpu_custom_call" | custom-call | bytes 3000000 | tf_op jit(solution)/shard_map/pallas_call | solution.py:708
  15.1 0.6 %shard_map.86 = (f32[2,6,48,384]{3,2,1,0:T(8,128)S(1)}, f32[3,2,48,384]{3,2,1,0:T(8,128)S(1)}, f32[3,2,48,384]{3,2,1,0:T(8,128)S(1)}, f32[2,3,48,384]{3,2,1,0:T(...) custom-call(f32[3,8,32,256]{3,2,1,0:T(8,128)S(1)} %get-tuple-element, ...), custom_call_target="tpu_custom_call", output_to_operand_aliasing={{0}: (8, {}), {1}: (9, {}), {2}: (10, {}), {3}: (11, {})} | custom-call | bytes 3000000 | tf_op jit(solution)/shard_map/pallas_call | solution.py:708
  15.7 4.6 %collective-permute-start.8 = (f32[7,32,256]{2,1,0:T(8,128)S(1)}, f32[7,32,256]{2,1,0:T(8,128)S(1)}, u32[]{:S(2)}, u32[]{:S(2)}) collective-permute-start(f32[7,32,256]{2,1,0:T(8,128)S(1)} %get-tuple-element.70), channel_id=1, source_target_pairs={{0,4},{8,12},{4,0},{12,8},{1,5},{9,13},{5,1},{13,9},{2,6},{10,14},... | collective-permute-start | bytes 688136 | tf_op jit(solution)/shard_map/ppermute | solution.py:789
  20.3 0.7 %collective-permute-start.9 = (f32[7,32,256]{2,1,0:T(8,128)S(1)}, f32[7,32,256]{2,1,0:T(8,128)S(1)}, u32[]{:S(2)}, u32[]{:S(2)}) collective-permute-start(f32[7,32,256]{2,1,0:T(8,128)S(1)} %get-tuple-element.71), channel_id=1, source_target_pairs={{4,8},{8,4},{5,9},{9,5},{6,10},{10,6},{7,11},{11,7},{20,24},{24,20... | collective-permute-start | bytes 688136 | tf_op jit(solution)/shard_map/ppermute | solution.py:790
  21.1 1.2 %collective-permute-done.6.xh = f32[32,128]{1,0:T(8,128)S(1)} collective-permute-done((f32[32,128]{1,0:T(8,128)S(1)}, f32[32,128]{1,0:T(8,128)S(1)}, u32[]{:S(2)}, u32[]{:S(2)}) %collective-permute-start.6) | collective-permute-done | bytes 16416 | tf_op jit(solution)/shard_map/ppermute | solution.py:791
  22.3 1.2 %collective-permute-start.7 = (f32[8,8,256]{2,1,0:T(8,128)S(1)}, f32[8,8,256]{2,1,0:T(8,128)S(1)}, u32[]{:S(2)}, u32[]{:S(2)}) collective-permute-start(f32[8,8,256]{2,1,0:T(8,128)S(1)} %shard_map.87.after.rest_0_), channel_id=1, source_target_pairs={{0,2},{2,0},{1,3},{3,1},{4,6},{6,4},{5,7},{7,5},{8,10},{10,8},{9,1... | collective-permute-start | bytes 196616 | tf_op jit(solution)/shard_map/ppermute | solution.py:795
  23.9 0.5 %shard_map.89 = (f32[3,8,48,384]{3,2,1,0:T(8,128)S(1)}, f32[8,48,384]{2,1,0:T(8,128)S(1)}, f32[6,6,48,384]{3,2,1,0:T(8,128)S(1)}) custom-call(f32[3,8,32,256]{3,2,1,0:T(8,128)S(1)} %get-tuple-element.67.u.refs_0_, f32[8,32,256]{2,1,0:T(8,128)S(1)} %get-tuple-element.68.d, f32[8,32,256]{2,1,0:T(8,128)S(1)} %copy-done, ...), custom_call_target="tpu_custom_call" | custom-call | bytes 3000000 | tf_op jit(solution)/shard_map/pallas_call | solution.py:708
  24.5 1.8 %collective-permute-done.8.first.refs_1_ = f32[7,32,256]{2,1,0:T(8,128)S(1)} collective-permute-done((f32[7,32,256]{2,1,0:T(8,128)S(1)}, f32[7,32,256]{2,1,0:T(8,128)S(1)}, u32[]{:S(2)}, u32[]{:S(2)}) %collective-permute-start.8) | collective-permute-done | bytes 229408 | tf_op jit(solution)/shard_map/ppermute | solution.py:789
  26.5 0.6 %collective-permute-start.11 = (f32[8,256]{1,0:T(8,128)S(1)}, f32[8,256]{1,0:T(8,128)S(1)}, u32[]{:S(2)}, u32[]{:S(2)}) collective-permute-start(f32[8,256]{1,0:T(8,128)S(1)} %shard_map.90.after), channel_id=1, source_target_pairs={{0,2},{2,0},{1,3},{3,1},{4,6},{6,4},{5,7},{7,5},{8,10},{10,8},{9,1... | collective-permute-start | bytes 24584 | tf_op jit(solution)/shard_map/ppermute | solution.py:840
  27.1 0.6 %shard_map.92 = (f32[3,8,48,384]{3,2,1,0:T(8,128)S(1)}, f32[8,48,384]{2,1,0:T(8,128)S(1)}, f32[6,6,48,384]{3,2,1,0:T(8,128)S(1)}) custom-call(f32[8,32,256]{2,1,0:T(8,128)S(1)} %copy-done, f32[8,8,256]{2,1,0:T(8,128)S(1)} %collective-permute-done.7.ylo.yhi, ...), custom_call_target="tpu_custom_call", output_to_operand_aliasing={{0}: (4, {}), {1}: (5, {}), {2}: (6, {})} | custom-call | bytes 6000000 | tf_op jit(solution)/shard_map/pallas_call | solution.py:708
  27.7 0.5 shard_map.93
  28.9 1.3 %collective-permute-done.11.refs_3_.refs_4_ = f32[8,256]{1,0:T(8,128)S(1)} collective-permute-done((f32[8,256]{1,0:T(8,128)S(1)}, f32[8,256]{1,0:T(8,128)S(1)}, u32[]{:S(2)}, u32[]{:S(2)}) %collective-permute-start.11) | collective-permute-done | bytes 8224 | tf_op jit(solution)/shard_map/ppermute | solution.py:840
  30.2 1.0 %shard_map.96 = (f32[2,6,48,384]{3,2,1,0:T(8,128)S(1)}, f32[3,2,48,384]{3,2,1,0:T(8,128)S(1)}, f32[3,2,48,384]{3,2,1,0:T(8,128)S(1)}, f32[2,3,48,384]{3,2,1,0:T(...) custom-call(f32[3,8,32,256]{3,2,1,0:T(8,128)S(1)} %get-tuple-element, ...), custom_call_target="tpu_custom_call", output_to_operand_aliasing={{0}: (8, {}), {1}: (9, {}), {2}: (10, {}), {3}: (11, {})} | custom-call | bytes 3000000 | tf_op jit(solution)/shard_map/pallas_call | solution.py:708
  31.3 1.2 %collective-permute-done.12 = f32[3,4,8,128]{3,2,1,0:T(8,128)S(1)} collective-permute-done((f32[3,4,8,128]{3,2,1,0:T(8,128)S(1)}, f32[3,4,8,128]{3,2,1,0:T(8,128)S(1)}, u32[]{:S(2)}, u32[]{:S(2)}) %collective-permute-start.12) | collective-permute-done | bytes 49184 | tf_op jit(solution)/shard_map/ppermute | solution.py:735
  32.5 0.6 %collective-permute-start.13 = (f32[3,4,8,128]{3,2,1,0:T(8,128)S(1)}, f32[3,4,8,128]{3,2,1,0:T(8,128)S(1)}, u32[]{:S(2)}, u32[]{:S(2)}) collective-permute-start(f32[3,4,8,128]{3,2,1,0:T(8,128)S(1)} %add.6), channel_id=1, source_target_pairs={{0,2},{2,0},{1,3},{3,1},{4,6},{6,4},{5,7},{7,5},{8,10},{10,8},{9,1... | collective-permute-start | bytes 147464 | tf_op jit(solution)/shard_map/ppermute | solution.py:735
  33.1 3.6 %collective-permute-done.13 = f32[3,4,8,128]{3,2,1,0:T(8,128)S(1)} collective-permute-done((f32[3,4,8,128]{3,2,1,0:T(8,128)S(1)}, f32[3,4,8,128]{3,2,1,0:T(8,128)S(1)}, u32[]{:S(2)}, u32[]{:S(2)}) %collective-permute-start.13) | collective-permute-done | bytes 49184 | tf_op jit(solution)/shard_map/ppermute | solution.py:735
  36.7 3.7 %collective-permute-start.14 = (f32[3,4,8,128]{3,2,1,0:T(8,128)S(1)}, f32[3,4,8,128]{3,2,1,0:T(8,128)S(1)}, u32[]{:S(2)}, u32[]{:S(2)}) collective-permute-start(f32[3,4,8,128]{3,2,1,0:T(8,128)S(1)} %add.7.refs_0_), channel_id=1, source_target_pairs={{0,4},{4,0},{8,12},{12,8},{1,5},{5,1},{9,13},{13,9},{2,6},{6,2},{1... | collective-permute-start | bytes 147464 | tf_op jit(solution)/shard_map/ppermute | solution.py:745
  40.4 1.2 %collective-permute-start.15 = (f32[3,4,8,128]{3,2,1,0:T(8,128)S(1)}, f32[3,4,8,128]{3,2,1,0:T(8,128)S(1)}, u32[]{:S(2)}, u32[]{:S(2)}) collective-permute-start(f32[3,4,8,128]{3,2,1,0:T(8,128)S(1)} %add.7.refs_0_), channel_id=1, source_target_pairs={{0,8},{4,12},{8,0},{12,4},{1,9},{5,13},{9,1},{13,5},{2,10},{6,14},... | collective-permute-start | bytes 147464 | tf_op jit(solution)/shard_map/ppermute | solution.py:745
  41.6 1.4 %collective-permute-start.16 = (f32[3,4,8,128]{3,2,1,0:T(8,128)S(1)}, f32[3,4,8,128]{3,2,1,0:T(8,128)S(1)}, u32[]{:S(2)}, u32[]{:S(2)}) collective-permute-start(f32[3,4,8,128]{3,2,1,0:T(8,128)S(1)} %add.7.refs_0_), channel_id=1, source_target_pairs={{0,12},{4,8},{8,4},{12,0},{1,13},{5,9},{9,5},{13,1},{2,14},{6,10},... | collective-permute-start | bytes 147464 | tf_op jit(solution)/shard_map/ppermute | solution.py:745
  43.0 0.9 %shard_map.97 = f32[3,8,32,256]{3,2,1,0:T(8,128)} custom-call(f32[3,4,32,256]{3,2,1,0:T(8,128)S(1)} %get-tuple-element.76.inner_moved, f32[3,2,32,256]{3,2,1,0:T(8,128)S(1)} %get-tuple-element.79.near_moved, f32[3,2,16,256]{3,2,1,0:T(8,128)S(1)} %get-tuple-element.81.mid_moved, f32[3,2,16,256]{3,2,1,0:T(8,128)S(1)} %get-tuple-element.89.edge_moved), custom_call_target="tpu_custom_call" | custom-call | bytes 3000000 | tf_op jit(solution)/shard_map/pallas_call | solution.py:708
  44.0 2.4 %shard_map.98 = f32[8,32,256]{2,1,0:T(8,128)} custom-call(f32[3,8,48,384]{3,2,1,0:T(8,128)S(1)} %get-tuple-element.77.U.refs_5_, f32[8,48,384]{2,1,0:T(8,128)S(1)} %get-tuple-element.78.D.refs_6_, f32[8,32,256]{2,1,0:T(8,128)S(1)} %copy-done, f32[7,32,256]{2,1,0:T(8,128)S(1)} %collective-permute-done.8.first.refs_1_, ...), custom_call_target="tpu_custom_call" | custom-call | bytes 6000000 | tf_op jit(solution)/shard_map/pallas_call | solution.py:708
  46.4 1.2 %collective-permute-done.16.refs_3_ = f32[3,4,8,128]{3,2,1,0:T(8,128)S(1)} collective-permute-done((f32[3,4,8,128]{3,2,1,0:T(8,128)S(1)}, f32[3,4,8,128]{3,2,1,0:T(8,128)S(1)}, u32[]{:S(2)}, u32[]{:S(2)}) %collective-permute-start.16) | collective-permute-done | bytes 49184 | tf_op jit(solution)/shard_map/ppermute | solution.py:745
  47.6 0.7 %shard_map.99 = f32[3,4096]{1,0:T(4,128)} custom-call(f32[3,4,8,128]{3,2,1,0:T(8,128)S(1)} %add.7.refs_0_, f32[3,4,8,128]{3,2,1,0:T(8,128)S(1)} %collective-permute-done.14.refs_1_, f32[3,4,8,128]{3,2,1,0:T(8,128)S(1)} %collective-permute-done.15.refs_2_, f32[3,4,8,128]{3,2,1,0:T(8,128)S(1)} %collective-permute-done.16.refs_3_), custom_call_target="tpu_custom_call" | custom-call | bytes 3000000 | tf_op jit(solution)/shard_map/pallas_call | solution.py:708
  (34 shorter events, 2.8 us)
Async XLA Ops:
  0.6 8.2 %copy-start = (f32[8,32,256]{2,1,0:T(8,128)S(1)}, f32[8,32,256]{2,1,0:T(8,128)}, u32[]{:S(2)}) copy-start(f32[8,32,256]{2,1,0:T(8,128)} %tough.13) | copy-start | bytes 786436
  2.0 8.7 %collective-permute-start = (f32[7,32,256]{2,1,0:T(8,128)S(1)}, f32[7,32,256]{2,1,0:T(8,128)S(1)}, u32[]{:S(2)}, u32[]{:S(2)}) collective-permute-start(f32[7,32,256]{2,1,0:T(8,128)S(1)} %get-tuple-element.48.first), channel_id=1, source_target_pairs={{0,4},{8,12},{4,0},{12,8},{1,5},{9,13},{5,1},{13,9},{2,6},{10,14},... | collective-permute-start | bytes 688136 | tf_op jit(solution)/shard_map/ppermute | solution.py:789
  5.1 5.6 %collective-permute-start.1 = (f32[7,32,256]{2,1,0:T(8,128)S(1)}, f32[7,32,256]{2,1,0:T(8,128)S(1)}, u32[]{:S(2)}, u32[]{:S(2)}) collective-permute-start(f32[7,32,256]{2,1,0:T(8,128)S(1)} %get-tuple-element.49), channel_id=1, source_target_pairs={{4,8},{8,4},{5,9},{9,5},{6,10},{10,6},{7,11},{11,7},{20,24},{24,20... | collective-permute-start | bytes 688136 | tf_op jit(solution)/shard_map/ppermute | solution.py:790
  6.0 1.2 %collective-permute-start.2 = (f32[32,128]{1,0:T(8,128)S(1)}, f32[32,128]{1,0:T(8,128)S(1)}, u32[]{:S(2)}, u32[]{:S(2)}) collective-permute-start(f32[32,128]{1,0:T(8,128)S(1)} %shard_map.77), channel_id=1, source_target_pairs={{0,1},{1,0},{2,3},{3,2},{4,5},{5,4},{6,7},{7,6},{8,9},{9,8},{10,11... | collective-permute-start | bytes 49160 | tf_op jit(solution)/shard_map/ppermute | solution.py:791
  7.3 5.4 %collective-permute-start.4 = (f32[8,8,256]{2,1,0:T(8,128)S(1)}, f32[8,8,256]{2,1,0:T(8,128)S(1)}, u32[]{:S(2)}, u32[]{:S(2)}) collective-permute-start(f32[8,8,256]{2,1,0:T(8,128)S(1)} %shard_map.78.rest_0_), channel_id=1, source_target_pairs={{0,2},{2,0},{1,3},{3,1},{4,6},{6,4},{5,7},{7,5},{8,10},{10,8},{9,1... | collective-permute-start | bytes 196616 | tf_op jit(solution)/shard_map/ppermute | solution.py:795
  10.9 3.8 %collective-permute-start.5 = (f32[32,128]{1,0:T(8,128)S(1)}, f32[32,128]{1,0:T(8,128)S(1)}, u32[]{:S(2)}, u32[]{:S(2)}) collective-permute-start(f32[32,128]{1,0:T(8,128)S(1)} %shard_map.81.after), channel_id=1, source_target_pairs={{0,1},{1,0},{2,3},{3,2},{4,5},{5,4},{6,7},{7,6},{8,9},{9,8},{10,11... | collective-permute-start | bytes 49160 | tf_op jit(solution)/shard_map/ppermute | solution.py:841
  10.9 4.2 %collective-permute-start.3 = (f32[8,256]{1,0:T(8,128)S(1)}, f32[8,256]{1,0:T(8,128)S(1)}, u32[]{:S(2)}, u32[]{:S(2)}) collective-permute-start(f32[8,256]{1,0:T(8,128)S(1)} %shard_map.80.after), channel_id=1, source_target_pairs={{0,2},{2,0},{1,3},{3,1},{4,6},{6,4},{5,7},{7,5},{8,10},{10,8},{9,1... | collective-permute-start | bytes 24584 | tf_op jit(solution)/shard_map/ppermute | solution.py:840
  15.1 8.4 %copy-start.1 = (bf16[8,32,1,4096]{3,1,2,0:T(8,128)(2,1)S(1)}, bf16[8,32,1,4096]{3,1,2,0:T(8,128)(2,1)}, u32[]{:S(2)}) copy-start(bf16[8,32,1,4096]{3,1,2,0:T(8,128)(2,1)} %param.8) | copy-start | bytes 6291460
  15.1 8.4 %copy-start.2 = (s32[4096]{0:T(1024)S(1)}, s32[4096]{0:T(1024)}, u32[]{:S(2)}) copy-start(s32[4096]{0:T(1024)} %param.9) | copy-start | bytes 49156
  15.7 10.5 %collective-permute-start.8 = (f32[7,32,256]{2,1,0:T(8,128)S(1)}, f32[7,32,256]{2,1,0:T(8,128)S(1)}, u32[]{:S(2)}, u32[]{:S(2)}) collective-permute-start(f32[7,32,256]{2,1,0:T(8,128)S(1)} %get-tuple-element.70), channel_id=1, source_target_pairs={{0,4},{8,12},{4,0},{12,8},{1,5},{9,13},{5,1},{13,9},{2,6},{10,14},... | collective-permute-start | bytes 688136 | tf_op jit(solution)/shard_map/ppermute | solution.py:789
  20.3 5.9 %collective-permute-start.9 = (f32[7,32,256]{2,1,0:T(8,128)S(1)}, f32[7,32,256]{2,1,0:T(8,128)S(1)}, u32[]{:S(2)}, u32[]{:S(2)}) collective-permute-start(f32[7,32,256]{2,1,0:T(8,128)S(1)} %get-tuple-element.71), channel_id=1, source_target_pairs={{4,8},{8,4},{5,9},{9,5},{6,10},{10,6},{7,11},{11,7},{20,24},{24,20... | collective-permute-start | bytes 688136 | tf_op jit(solution)/shard_map/ppermute | solution.py:790
  21.0 1.2 %collective-permute-start.6 = (f32[32,128]{1,0:T(8,128)S(1)}, f32[32,128]{1,0:T(8,128)S(1)}, u32[]{:S(2)}, u32[]{:S(2)}) collective-permute-start(f32[32,128]{1,0:T(8,128)S(1)} %get-tuple-element.69), channel_id=1, source_target_pairs={{0,1},{1,0},{2,3},{3,2},{4,5},{5,4},{6,7},{7,6},{8,9},{9,8},{10,11... | collective-permute-start | bytes 49160 | tf_op jit(solution)/shard_map/ppermute | solution.py:791
  22.3 4.8 %collective-permute-start.7 = (f32[8,8,256]{2,1,0:T(8,128)S(1)}, f32[8,8,256]{2,1,0:T(8,128)S(1)}, u32[]{:S(2)}, u32[]{:S(2)}) collective-permute-start(f32[8,8,256]{2,1,0:T(8,128)S(1)} %shard_map.87.after.rest_0_), channel_id=1, source_target_pairs={{0,2},{2,0},{1,3},{3,1},{4,6},{6,4},{5,7},{7,5},{8,10},{10,8},{9,1... | collective-permute-start | bytes 196616 | tf_op jit(solution)/shard_map/ppermute | solution.py:795
  26.5 2.1 %collective-permute-start.10 = (f32[32,128]{1,0:T(8,128)S(1)}, f32[32,128]{1,0:T(8,128)S(1)}, u32[]{:S(2)}, u32[]{:S(2)}) collective-permute-start(f32[32,128]{1,0:T(8,128)S(1)} %shard_map.91.after), channel_id=1, source_target_pairs={{0,1},{1,0},{2,3},{3,2},{4,5},{5,4},{6,7},{7,6},{8,9},{9,8},{10,11... | collective-permute-start | bytes 49160 | tf_op jit(solution)/shard_map/ppermute | solution.py:841
  26.5 3.7 %collective-permute-start.11 = (f32[8,256]{1,0:T(8,128)S(1)}, f32[8,256]{1,0:T(8,128)S(1)}, u32[]{:S(2)}, u32[]{:S(2)}) collective-permute-start(f32[8,256]{1,0:T(8,128)S(1)} %shard_map.90.after), channel_id=1, source_target_pairs={{0,2},{2,0},{1,3},{3,1},{4,6},{6,4},{5,7},{7,5},{8,10},{10,8},{9,1... | collective-permute-start | bytes 24584 | tf_op jit(solution)/shard_map/ppermute | solution.py:840
  31.2 1.3 %collective-permute-start.12 = (f32[3,4,8,128]{3,2,1,0:T(8,128)S(1)}, f32[3,4,8,128]{3,2,1,0:T(8,128)S(1)}, u32[]{:S(2)}, u32[]{:S(2)}) collective-permute-start(f32[3,4,8,128]{3,2,1,0:T(8,128)S(1)} %get-tuple-element.90.after), channel_id=1, source_target_pairs={{0,1},{1,0},{2,3},{3,2},{4,5},{5,4},{6,7},{7,6},{8,9},{9,8},{10,11... | collective-permute-start | bytes 147464 | tf_op jit(solution)/shard_map/ppermute | solution.py:735
  32.5 4.2 %collective-permute-start.13 = (f32[3,4,8,128]{3,2,1,0:T(8,128)S(1)}, f32[3,4,8,128]{3,2,1,0:T(8,128)S(1)}, u32[]{:S(2)}, u32[]{:S(2)}) collective-permute-start(f32[3,4,8,128]{3,2,1,0:T(8,128)S(1)} %add.6), channel_id=1, source_target_pairs={{0,2},{2,0},{1,3},{3,1},{4,6},{6,4},{5,7},{7,5},{8,10},{10,8},{9,1... | collective-permute-start | bytes 147464 | tf_op jit(solution)/shard_map/ppermute | solution.py:735
  36.7 9.7 %collective-permute-start.14 = (f32[3,4,8,128]{3,2,1,0:T(8,128)S(1)}, f32[3,4,8,128]{3,2,1,0:T(8,128)S(1)}, u32[]{:S(2)}, u32[]{:S(2)}) collective-permute-start(f32[3,4,8,128]{3,2,1,0:T(8,128)S(1)} %add.7.refs_0_), channel_id=1, source_target_pairs={{0,4},{4,0},{8,12},{12,8},{1,5},{5,1},{9,13},{13,9},{2,6},{6,2},{1... | collective-permute-start | bytes 147464 | tf_op jit(solution)/shard_map/ppermute | solution.py:745
  40.4 6.0 %collective-permute-start.15 = (f32[3,4,8,128]{3,2,1,0:T(8,128)S(1)}, f32[3,4,8,128]{3,2,1,0:T(8,128)S(1)}, u32[]{:S(2)}, u32[]{:S(2)}) collective-permute-start(f32[3,4,8,128]{3,2,1,0:T(8,128)S(1)} %add.7.refs_0_), channel_id=1, source_target_pairs={{0,8},{4,12},{8,0},{12,4},{1,9},{5,13},{9,1},{13,5},{2,10},{6,14},... | collective-permute-start | bytes 147464 | tf_op jit(solution)/shard_map/ppermute | solution.py:745
  41.6 6.0 %collective-permute-start.16 = (f32[3,4,8,128]{3,2,1,0:T(8,128)S(1)}, f32[3,4,8,128]{3,2,1,0:T(8,128)S(1)}, u32[]{:S(2)}, u32[]{:S(2)}) collective-permute-start(f32[3,4,8,128]{3,2,1,0:T(8,128)S(1)} %add.7.refs_0_), channel_id=1, source_target_pairs={{0,12},{4,8},{8,4},{12,0},{1,13},{5,9},{9,5},{13,1},{2,14},{6,10},... | collective-permute-start | bytes 147464 | tf_op jit(solution)/shard_map/ppermute | solution.py:745
